TPU v7x, 512 devices: a whole 4x8x8 slice. The times are simulated.
512 devices in a mesh: sweep: 16 (over z, core), lat: 32 (over y, x).
Axes of the slice: x: 4, y: 8, z: 8, core: 2. Of those that a mesh axis runs over, the one named last changes fastest.
Arguments:
- traveltime: float32 [2, 128, 512, 384], P(None, 'sweep', 'lat'), may hold values from 0 to 4
- residual: float32 [2, 128, 512, 384], P(None, 'sweep', 'lat'), may hold values from -6 to 6
- slowness: float32 [128, 512, 384], P('sweep', 'lat'), may hold values from 0.3 to 0.6
- attenuation: float32 [128, 512, 384], P('sweep', 'lat'), may hold values from 0.005 to 0.05
- topography: int32 [512, 384], P('lat'), may hold values from 0 to 127, as said below
Outputs:
- adjoint: float32 [2, 128, 512, 384], P(None, 'sweep', 'lat')
- gradient: float32 [128, 512, 384], P('sweep', 'lat')
Inputs may be any that keep to these rules, and one draw needn't show every extreme that they name: Apart from two corner columns, topography is a level shared by each aligned strip of 16 columns along the first lateral dimension plus a small rough offset per column, so that whole blocks of planes lie above it; the first column of the grid has topography 128 - 1 and the last column 0.
All inputs are finite; a program needn't handle non-finite values.
Results may differ from a plain program's by a relative error of at most 0.0003.
Values sent between devices are 32-bit elements; how exact they have to be, the bound alone decides.
No kernel may reach another device: no remote copies, remote signals or barrier semaphores. Data moves between devices by JAX's collectives and lax.ppermute only.
A program may use at most 64 MiB of HBM per device.

v0:
```python
import jax
import jax.numpy as jnp
from jax import lax
from jax.sharding import PartitionSpec as P


def extended(cells, sides, width):
    for axis, dim in sides:
        count = lax.axis_size(axis)
        ends = count - 1
        head = lax.slice_in_dim(cells, 0, width, axis=dim)
        tail = lax.slice_in_dim(cells, cells.shape[dim] - width, cells.shape[dim], axis=dim)
        cells = jnp.concatenate(
            [
                lax.ppermute(tail, axis, [(i, (i + 1) % count) for i in range(ends)]),
                cells,
                lax.ppermute(head, axis, [((i + 1) % count, i) for i in range(ends)]),
            ],
            axis=dim,
        )
    return cells


def shifted(block, axis, distance):
    devices = range(lax.axis_size(axis))
    route = [(i - distance, i) for i in devices if i - distance in devices]
    return lax.ppermute(block, axis, route)


def shift_low(field, along):
    count = field.shape[along]
    padding = jnp.zeros_like(lax.slice_in_dim(field, 0, 1, axis=along))
    return jnp.concatenate([padding, lax.slice_in_dim(field, 0, count - 1, axis=along)], axis=along)


def shift_high(field, along):
    count = field.shape[along]
    padding = jnp.zeros_like(lax.slice_in_dim(field, 0, 1, axis=along))
    return jnp.concatenate([lax.slice_in_dim(field, 1, count, axis=along), padding], axis=along)


def upwind_weights(tau_wide):
    last = tau_wide.ndim - 1
    center = tau_wide[..., 1:-1, :]
    west = jax.nn.softplus(center - tau_wide[..., :-2, :])
    east = jax.nn.softplus(center - tau_wide[..., 2:, :])
    north = jax.nn.softplus(center - shift_low(center, last))
    south = jax.nn.softplus(center - shift_high(center, last))
    return (west, east, north, south)


def shards(traveltime, residual, slowness, attenuation, topography):
    sources, planes, columns, crosses = traveltime.shape
    plane_index = lax.axis_index("sweep") * planes + lax.iota(jnp.int32, planes)
    active = (plane_index[:, None, None] >= topography[None]).astype(jnp.float32)
    tau_wide = extended(traveltime, (("lat", 2),), 1)
    west, east, north, south = upwind_weights(tau_wide)
    denominator = slowness + west + east + north + south + attenuation
    scale = active / denominator
    packed = jnp.concatenate([residual, west, east, north, south, scale, slowness[None]], axis=0)
    widened = extended(packed, (("lat", 2),), planes)
    source_w = widened[0:sources]
    west_w = widened[sources : 2 * sources]
    east_w = widened[2 * sources : 3 * sources]
    north_w = widened[3 * sources : 4 * sources]
    south_w = widened[4 * sources : 5 * sources]
    scale_w = widened[5 * sources : 6 * sources]
    slow_w = widened[6 * sources]

    def update_block(previous):
        results = []
        for level in range(planes):
            current = scale_w[:, level] * (
                source_w[:, level]
                + slow_w[level] * previous
                + west_w[:, level] * shift_low(previous, 1)
                + east_w[:, level] * shift_high(previous, 1)
                + north_w[:, level] * shift_low(previous, 2)
                + south_w[:, level] * shift_high(previous, 2)
            )
            results.append(current[:, planes : planes + columns])
            previous = current
        return jnp.stack(results, axis=1)

    def advance(counter, carried):
        inflow, current_block = carried
        previous = extended(inflow, (("lat", 1),), planes)
        new_block = update_block(previous)
        new_inflow = shifted(new_block[:, -1], "sweep", 1)
        return (new_inflow, new_block)

    start = (
        jnp.zeros((sources, columns, crosses), jnp.float32),
        jnp.zeros((sources, planes, columns, crosses), jnp.float32),
    )
    _, adjoint = lax.fori_loop(0, lax.axis_size("sweep"), advance, start)
    gradient = slowness * jnp.sum(adjoint, axis=0)
    return (adjoint, gradient)


def solution(mesh):
    in_specs = (
        P(None, "sweep", "lat", None),
        P(None, "sweep", "lat", None),
        P("sweep", "lat", None),
        P("sweep", "lat", None),
        P("lat", None),
    )
    out_specs = (P(None, "sweep", "lat", None), P("sweep", "lat", None))
    return jax.shard_map(shards, mesh=mesh, in_specs=in_specs, out_specs=out_specs, check_vma=False)
```

profile of v0, /device:TPU:223, one launch (start us, length us, event | category | flops | bytes accessed | tf_op | source)
XLA Modules:
  0.0 528.2 jit_solution(7345833304145075806)
XLA Ops:
  2.4 4.3 collective-permute-start.3
  20.0 5.4 %collective-permute-start.5 = (f32[13,8,8,384]{3,2,0,1:T(8,128)}, f32[13,8,8,384]{3,2,0,1:T(8,128)}, u32[]{:S(2)}, u32[]{:S(2)}) collective-permute-start(f32[13,8,8,384]{3,2,0,1:T(8,128)} %get-tuple-element.134), channel_id=1, source_target_pairs={{0,1},{1,2},{2,3},{3,4},{4,5},{5,6},{6,7},{7,8},{8,9},{9,10},{10,1... | collective-permute-start | bytes 3833864 | tf_op jit(solution)/shard_map/ppermute | solution.py:15
  27.4 24.5 %collective-permute-done.5 = f32[13,8,8,384]{3,2,0,1:T(8,128)} collective-permute-done((f32[13,8,8,384]{3,2,0,1:T(8,128)}, f32[13,8,8,384]{3,2,0,1:T(8,128)}, u32[]{:S(2)}, u32[]{:S(2)}) %collective-permute-start.5) | collective-permute-done | bytes 1277984 | tf_op jit(solution)/shard_map/ppermute | solution.py:15
  52.0 7.2 %collective-permute-done.6 = f32[13,8,8,384]{3,2,0,1:T(8,128)} collective-permute-done((f32[13,8,8,384]{3,2,0,1:T(8,128)}, f32[13,8,8,384]{3,2,0,1:T(8,128)}, u32[]{:S(2)}, u32[]{:S(2)}) %collective-permute-start.6) | collective-permute-done | bytes 1277984 | tf_op jit(solution)/shard_map/ppermute | solution.py:17
  62.3 3.7 pad_maximum_fusion.1
  66.0 458.7 %while.13 = (s32[]{:T(128)}, f32[2,16,384]{2,1,0:T(8,128)S(1)}, f32[2,8,16,384]{3,2,0,1:T(8,128)}, f32[2,8,32,384]{3,2,0,1:T(8,128)}, f32[2,8,32,384]{3,2,0,1:T(...) while((s32[]{:T(128)}, f32[2,16,384]{2,1,0:T(8,128)S(1)}, ...), condition=%wide.region_1.2_spmd.clone, body=%wide.region_0.1_spmd.sunk.clone | while | flops 2039810 | bytes 20638456 | solution.py:96
  67.9 3.4 collective-permute-start.1
  85.7 8.6 %collective-permute-start.2 = (f32[2,16,384]{2,1,0:T(8,128)S(1)}, f32[2,16,384]{2,1,0:T(8,128)S(1)}, u32[]{:S(2)}, u32[]{:S(2)}) collective-permute-start(f32[2,16,384]{2,1,0:T(8,128)S(1)} %get-tuple-element.365), channel_id=1, source_target_pairs={{0,32},{32,64},{64,96},{96,128},{128,160},{160,192},{192,224},{224... | collective-permute-start | bytes 147464 | tf_op jit(solution)/shard_map/while/body/eval_jaxpr/ppermute | solution.py:27
  103.7 2.8 collective-permute-done.1
  116.3 6.5 %collective-permute-start.2 = (f32[2,16,384]{2,1,0:T(8,128)S(1)}, f32[2,16,384]{2,1,0:T(8,128)S(1)}, u32[]{:S(2)}, u32[]{:S(2)}) collective-permute-start(f32[2,16,384]{2,1,0:T(8,128)S(1)} %get-tuple-element.365), channel_id=1, source_target_pairs={{0,32},{32,64},{64,96},{96,128},{128,160},{160,192},{192,224},{224... | collective-permute-start | bytes 147464 | tf_op jit(solution)/shard_map/while/body/eval_jaxpr/ppermute | solution.py:27
  144.6 6.9 %collective-permute-start.2 = (f32[2,16,384]{2,1,0:T(8,128)S(1)}, f32[2,16,384]{2,1,0:T(8,128)S(1)}, u32[]{:S(2)}, u32[]{:S(2)}) collective-permute-start(f32[2,16,384]{2,1,0:T(8,128)S(1)} %get-tuple-element.365), channel_id=1, source_target_pairs={{0,32},{32,64},{64,96},{96,128},{128,160},{160,192},{192,224},{224... | collective-permute-start | bytes 147464 | tf_op jit(solution)/shard_map/while/body/eval_jaxpr/ppermute | solution.py:27
  173.2 6.9 %collective-permute-start.2 = (f32[2,16,384]{2,1,0:T(8,128)S(1)}, f32[2,16,384]{2,1,0:T(8,128)S(1)}, u32[]{:S(2)}, u32[]{:S(2)}) collective-permute-start(f32[2,16,384]{2,1,0:T(8,128)S(1)} %get-tuple-element.365), channel_id=1, source_target_pairs={{0,32},{32,64},{64,96},{96,128},{128,160},{160,192},{192,224},{224... | collective-permute-start | bytes 147464 | tf_op jit(solution)/shard_map/while/body/eval_jaxpr/ppermute | solution.py:27
  201.8 6.9 %collective-permute-start.2 = (f32[2,16,384]{2,1,0:T(8,128)S(1)}, f32[2,16,384]{2,1,0:T(8,128)S(1)}, u32[]{:S(2)}, u32[]{:S(2)}) collective-permute-start(f32[2,16,384]{2,1,0:T(8,128)S(1)} %get-tuple-element.365), channel_id=1, source_target_pairs={{0,32},{32,64},{64,96},{96,128},{128,160},{160,192},{192,224},{224... | collective-permute-start | bytes 147464 | tf_op jit(solution)/shard_map/while/body/eval_jaxpr/ppermute | solution.py:27
  230.5 6.9 %collective-permute-start.2 = (f32[2,16,384]{2,1,0:T(8,128)S(1)}, f32[2,16,384]{2,1,0:T(8,128)S(1)}, u32[]{:S(2)}, u32[]{:S(2)}) collective-permute-start(f32[2,16,384]{2,1,0:T(8,128)S(1)} %get-tuple-element.365), channel_id=1, source_target_pairs={{0,32},{32,64},{64,96},{96,128},{128,160},{160,192},{192,224},{224... | collective-permute-start | bytes 147464 | tf_op jit(solution)/shard_map/while/body/eval_jaxpr/ppermute | solution.py:27
  259.1 6.9 %collective-permute-start.2 = (f32[2,16,384]{2,1,0:T(8,128)S(1)}, f32[2,16,384]{2,1,0:T(8,128)S(1)}, u32[]{:S(2)}, u32[]{:S(2)}) collective-permute-start(f32[2,16,384]{2,1,0:T(8,128)S(1)} %get-tuple-element.365), channel_id=1, source_target_pairs={{0,32},{32,64},{64,96},{96,128},{128,160},{160,192},{192,224},{224... | collective-permute-start | bytes 147464 | tf_op jit(solution)/shard_map/while/body/eval_jaxpr/ppermute | solution.py:27
  287.7 6.9 %collective-permute-start.2 = (f32[2,16,384]{2,1,0:T(8,128)S(1)}, f32[2,16,384]{2,1,0:T(8,128)S(1)}, u32[]{:S(2)}, u32[]{:S(2)}) collective-permute-start(f32[2,16,384]{2,1,0:T(8,128)S(1)} %get-tuple-element.365), channel_id=1, source_target_pairs={{0,32},{32,64},{64,96},{96,128},{128,160},{160,192},{192,224},{224... | collective-permute-start | bytes 147464 | tf_op jit(solution)/shard_map/while/body/eval_jaxpr/ppermute | solution.py:27
  316.3 6.9 %collective-permute-start.2 = (f32[2,16,384]{2,1,0:T(8,128)S(1)}, f32[2,16,384]{2,1,0:T(8,128)S(1)}, u32[]{:S(2)}, u32[]{:S(2)}) collective-permute-start(f32[2,16,384]{2,1,0:T(8,128)S(1)} %get-tuple-element.365), channel_id=1, source_target_pairs={{0,32},{32,64},{64,96},{96,128},{128,160},{160,192},{192,224},{224... | collective-permute-start | bytes 147464 | tf_op jit(solution)/shard_map/while/body/eval_jaxpr/ppermute | solution.py:27
  344.9 6.9 %collective-permute-start.2 = (f32[2,16,384]{2,1,0:T(8,128)S(1)}, f32[2,16,384]{2,1,0:T(8,128)S(1)}, u32[]{:S(2)}, u32[]{:S(2)}) collective-permute-start(f32[2,16,384]{2,1,0:T(8,128)S(1)} %get-tuple-element.365), channel_id=1, source_target_pairs={{0,32},{32,64},{64,96},{96,128},{128,160},{160,192},{192,224},{224... | collective-permute-start | bytes 147464 | tf_op jit(solution)/shard_map/while/body/eval_jaxpr/ppermute | solution.py:27
  373.5 6.9 %collective-permute-start.2 = (f32[2,16,384]{2,1,0:T(8,128)S(1)}, f32[2,16,384]{2,1,0:T(8,128)S(1)}, u32[]{:S(2)}, u32[]{:S(2)}) collective-permute-start(f32[2,16,384]{2,1,0:T(8,128)S(1)} %get-tuple-element.365), channel_id=1, source_target_pairs={{0,32},{32,64},{64,96},{96,128},{128,160},{160,192},{192,224},{224... | collective-permute-start | bytes 147464 | tf_op jit(solution)/shard_map/while/body/eval_jaxpr/ppermute | solution.py:27
  402.1 6.9 %collective-permute-start.2 = (f32[2,16,384]{2,1,0:T(8,128)S(1)}, f32[2,16,384]{2,1,0:T(8,128)S(1)}, u32[]{:S(2)}, u32[]{:S(2)}) collective-permute-start(f32[2,16,384]{2,1,0:T(8,128)S(1)} %get-tuple-element.365), channel_id=1, source_target_pairs={{0,32},{32,64},{64,96},{96,128},{128,160},{160,192},{192,224},{224... | collective-permute-start | bytes 147464 | tf_op jit(solution)/shard_map/while/body/eval_jaxpr/ppermute | solution.py:27
  430.8 6.9 %collective-permute-start.2 = (f32[2,16,384]{2,1,0:T(8,128)S(1)}, f32[2,16,384]{2,1,0:T(8,128)S(1)}, u32[]{:S(2)}, u32[]{:S(2)}) collective-permute-start(f32[2,16,384]{2,1,0:T(8,128)S(1)} %get-tuple-element.365), channel_id=1, source_target_pairs={{0,32},{32,64},{64,96},{96,128},{128,160},{160,192},{192,224},{224... | collective-permute-start | bytes 147464 | tf_op jit(solution)/shard_map/while/body/eval_jaxpr/ppermute | solution.py:27
  459.4 6.9 %collective-permute-start.2 = (f32[2,16,384]{2,1,0:T(8,128)S(1)}, f32[2,16,384]{2,1,0:T(8,128)S(1)}, u32[]{:S(2)}, u32[]{:S(2)}) collective-permute-start(f32[2,16,384]{2,1,0:T(8,128)S(1)} %get-tuple-element.365), channel_id=1, source_target_pairs={{0,32},{32,64},{64,96},{96,128},{128,160},{160,192},{192,224},{224... | collective-permute-start | bytes 147464 | tf_op jit(solution)/shard_map/while/body/eval_jaxpr/ppermute | solution.py:27
  488.0 6.9 %collective-permute-start.2 = (f32[2,16,384]{2,1,0:T(8,128)S(1)}, f32[2,16,384]{2,1,0:T(8,128)S(1)}, u32[]{:S(2)}, u32[]{:S(2)}) collective-permute-start(f32[2,16,384]{2,1,0:T(8,128)S(1)} %get-tuple-element.365), channel_id=1, source_target_pairs={{0,32},{32,64},{64,96},{96,128},{128,160},{160,192},{192,224},{224... | collective-permute-start | bytes 147464 | tf_op jit(solution)/shard_map/while/body/eval_jaxpr/ppermute | solution.py:27
  516.6 6.9 %collective-permute-start.2 = (f32[2,16,384]{2,1,0:T(8,128)S(1)}, f32[2,16,384]{2,1,0:T(8,128)S(1)}, u32[]{:S(2)}, u32[]{:S(2)}) collective-permute-start(f32[2,16,384]{2,1,0:T(8,128)S(1)} %get-tuple-element.365), channel_id=1, source_target_pairs={{0,32},{32,64},{64,96},{96,128},{128,160},{160,192},{192,224},{224... | collective-permute-start | bytes 147464 | tf_op jit(solution)/shard_map/while/body/eval_jaxpr/ppermute | solution.py:27
  (766 shorter events, 360.0 us)
Async XLA Ops:
  2.4 10.3 %collective-permute-start.3 = (f32[2,8,1,384]{3,2,0,1:T(1,128)}, f32[2,8,1,384]{3,2,0,1:T(1,128)}, u32[]{:S(2)}, u32[]{:S(2)}) collective-permute-start(f32[2,8,1,384]{3,2,0,1:T(1,128)} %get-tuple-element.139), channel_id=1, source_target_pairs={{0,1},{1,2},{2,3},{3,4},{4,5},{5,6},{6,7},{7,8},{8,9},{9,10},{10,1... | collective-permute-start | bytes 73736 | tf_op jit(solution)/shard_map/ppermute | solution.py:15
  6.7 8.2 %collective-permute-start.4 = (f32[2,8,1,384]{3,2,0,1:T(1,128)}, f32[2,8,1,384]{3,2,0,1:T(1,128)}, u32[]{:S(2)}, u32[]{:S(2)}) collective-permute-start(f32[2,8,1,384]{3,2,0,1:T(1,128)} %get-tuple-element.138), channel_id=1, source_target_pairs={{1,0},{2,1},{3,2},{4,3},{5,4},{6,5},{7,6},{8,7},{9,8},{10,9},{11,1... | collective-permute-start | bytes 73736 | tf_op jit(solution)/shard_map/ppermute | solution.py:17
  20.0 31.9 %collective-permute-start.5 = (f32[13,8,8,384]{3,2,0,1:T(8,128)}, f32[13,8,8,384]{3,2,0,1:T(8,128)}, u32[]{:S(2)}, u32[]{:S(2)}) collective-permute-start(f32[13,8,8,384]{3,2,0,1:T(8,128)} %get-tuple-element.134), channel_id=1, source_target_pairs={{0,1},{1,2},{2,3},{3,4},{4,5},{5,6},{6,7},{7,8},{8,9},{9,10},{10,1... | collective-permute-start | bytes 3833864 | tf_op jit(solution)/shard_map/ppermute | solution.py:15
  25.5 33.6 %collective-permute-start.6 = (f32[13,8,8,384]{3,2,0,1:T(8,128)}, f32[13,8,8,384]{3,2,0,1:T(8,128)}, u32[]{:S(2)}, u32[]{:S(2)}) collective-permute-start(f32[13,8,8,384]{3,2,0,1:T(8,128)} %get-tuple-element.135), channel_id=1, source_target_pairs={{1,0},{2,1},{3,2},{4,3},{5,4},{6,5},{7,6},{8,7},{9,8},{10,9},{11,1... | collective-permute-start | bytes 3833864 | tf_op jit(solution)/shard_map/ppermute | solution.py:17
  66.0 8.2 %collective-permute-start = (f32[2,8,384]{2,1,0:T(8,128)S(1)}, f32[2,8,384]{2,1,0:T(8,128)S(1)}, u32[]{:S(2)}, u32[]{:S(2)}) collective-permute-start(f32[2,8,384]{2,1,0:T(8,128)S(1)} %get-tuple-element.315), channel_id=1, source_target_pairs={{0,1},{1,2},{2,3},{3,4},{4,5},{5,6},{6,7},{7,8},{8,9},{9,10},{10,1... | collective-permute-start | bytes 73736 | tf_op jit(solution)/shard_map/while/body/eval_jaxpr/ppermute | solution.py:15
  85.7 9.8 %collective-permute-start.2 = (f32[2,16,384]{2,1,0:T(8,128)S(1)}, f32[2,16,384]{2,1,0:T(8,128)S(1)}, u32[]{:S(2)}, u32[]{:S(2)}) collective-permute-start(f32[2,16,384]{2,1,0:T(8,128)S(1)} %get-tuple-element.365), channel_id=1, source_target_pairs={{0,32},{32,64},{64,96},{96,128},{128,160},{160,192},{192,224},{224... | collective-permute-start | bytes 147464 | tf_op jit(solution)/shard_map/while/body/eval_jaxpr/ppermute | solution.py:27
  95.4 8.2 %collective-permute-start = (f32[2,8,384]{2,1,0:T(8,128)S(1)}, f32[2,8,384]{2,1,0:T(8,128)S(1)}, u32[]{:S(2)}, u32[]{:S(2)}) collective-permute-start(f32[2,8,384]{2,1,0:T(8,128)S(1)} %get-tuple-element.315), channel_id=1, source_target_pairs={{0,1},{1,2},{2,3},{3,4},{4,5},{5,6},{6,7},{7,8},{8,9},{9,10},{10,1... | collective-permute-start | bytes 73736 | tf_op jit(solution)/shard_map/while/body/eval_jaxpr/ppermute | solution.py:15
  98.3 8.2 %collective-permute-start.1 = (f32[2,8,384]{2,1,0:T(8,128)S(1)}, f32[2,8,384]{2,1,0:T(8,128)S(1)}, u32[]{:S(2)}, u32[]{:S(2)}) collective-permute-start(f32[2,8,384]{2,1,0:T(8,128)S(1)} %get-tuple-element.316), channel_id=1, source_target_pairs={{1,0},{2,1},{3,2},{4,3},{5,4},{6,5},{7,6},{8,7},{9,8},{10,9},{11,1... | collective-permute-start | bytes 73736 | tf_op jit(solution)/shard_map/while/body/eval_jaxpr/ppermute | solution.py:17
  124.1 8.2 %collective-permute-start = (f32[2,8,384]{2,1,0:T(8,128)S(1)}, f32[2,8,384]{2,1,0:T(8,128)S(1)}, u32[]{:S(2)}, u32[]{:S(2)}) collective-permute-start(f32[2,8,384]{2,1,0:T(8,128)S(1)} %get-tuple-element.315), channel_id=1, source_target_pairs={{0,1},{1,2},{2,3},{3,4},{4,5},{5,6},{6,7},{7,8},{8,9},{9,10},{10,1... | collective-permute-start | bytes 73736 | tf_op jit(solution)/shard_map/while/body/eval_jaxpr/ppermute | solution.py:15
  144.6 8.1 %collective-permute-start.2 = (f32[2,16,384]{2,1,0:T(8,128)S(1)}, f32[2,16,384]{2,1,0:T(8,128)S(1)}, u32[]{:S(2)}, u32[]{:S(2)}) collective-permute-start(f32[2,16,384]{2,1,0:T(8,128)S(1)} %get-tuple-element.365), channel_id=1, source_target_pairs={{0,32},{32,64},{64,96},{96,128},{128,160},{160,192},{192,224},{224... | collective-permute-start | bytes 147464 | tf_op jit(solution)/shard_map/while/body/eval_jaxpr/ppermute | solution.py:27
  152.7 8.2 %collective-permute-start = (f32[2,8,384]{2,1,0:T(8,128)S(1)}, f32[2,8,384]{2,1,0:T(8,128)S(1)}, u32[]{:S(2)}, u32[]{:S(2)}) collective-permute-start(f32[2,8,384]{2,1,0:T(8,128)S(1)} %get-tuple-element.315), channel_id=1, source_target_pairs={{0,1},{1,2},{2,3},{3,4},{4,5},{5,6},{6,7},{7,8},{8,9},{9,10},{10,1... | collective-permute-start | bytes 73736 | tf_op jit(solution)/shard_map/while/body/eval_jaxpr/ppermute | solution.py:15
  173.2 8.1 %collective-permute-start.2 = (f32[2,16,384]{2,1,0:T(8,128)S(1)}, f32[2,16,384]{2,1,0:T(8,128)S(1)}, u32[]{:S(2)}, u32[]{:S(2)}) collective-permute-start(f32[2,16,384]{2,1,0:T(8,128)S(1)} %get-tuple-element.365), channel_id=1, source_target_pairs={{0,32},{32,64},{64,96},{96,128},{128,160},{160,192},{192,224},{224... | collective-permute-start | bytes 147464 | tf_op jit(solution)/shard_map/while/body/eval_jaxpr/ppermute | solution.py:27
  181.3 8.2 %collective-permute-start = (f32[2,8,384]{2,1,0:T(8,128)S(1)}, f32[2,8,384]{2,1,0:T(8,128)S(1)}, u32[]{:S(2)}, u32[]{:S(2)}) collective-permute-start(f32[2,8,384]{2,1,0:T(8,128)S(1)} %get-tuple-element.315), channel_id=1, source_target_pairs={{0,1},{1,2},{2,3},{3,4},{4,5},{5,6},{6,7},{7,8},{8,9},{9,10},{10,1... | collective-permute-start | bytes 73736 | tf_op jit(solution)/shard_map/while/body/eval_jaxpr/ppermute | solution.py:15
  209.9 8.2 %collective-permute-start = (f32[2,8,384]{2,1,0:T(8,128)S(1)}, f32[2,8,384]{2,1,0:T(8,128)S(1)}, u32[]{:S(2)}, u32[]{:S(2)}) collective-permute-start(f32[2,8,384]{2,1,0:T(8,128)S(1)} %get-tuple-element.315), channel_id=1, source_target_pairs={{0,1},{1,2},{2,3},{3,4},{4,5},{5,6},{6,7},{7,8},{8,9},{9,10},{10,1... | collective-permute-start | bytes 73736 | tf_op jit(solution)/shard_map/while/body/eval_jaxpr/ppermute | solution.py:15
  238.5 8.2 %collective-permute-start = (f32[2,8,384]{2,1,0:T(8,128)S(1)}, f32[2,8,384]{2,1,0:T(8,128)S(1)}, u32[]{:S(2)}, u32[]{:S(2)}) collective-permute-start(f32[2,8,384]{2,1,0:T(8,128)S(1)} %get-tuple-element.315), channel_id=1, source_target_pairs={{0,1},{1,2},{2,3},{3,4},{4,5},{5,6},{6,7},{7,8},{8,9},{9,10},{10,1... | collective-permute-start | bytes 73736 | tf_op jit(solution)/shard_map/while/body/eval_jaxpr/ppermute | solution.py:15
  267.1 8.2 %collective-permute-start = (f32[2,8,384]{2,1,0:T(8,128)S(1)}, f32[2,8,384]{2,1,0:T(8,128)S(1)}, u32[]{:S(2)}, u32[]{:S(2)}) collective-permute-start(f32[2,8,384]{2,1,0:T(8,128)S(1)} %get-tuple-element.315), channel_id=1, source_target_pairs={{0,1},{1,2},{2,3},{3,4},{4,5},{5,6},{6,7},{7,8},{8,9},{9,10},{10,1... | collective-permute-start | bytes 73736 | tf_op jit(solution)/shard_map/while/body/eval_jaxpr/ppermute | solution.py:15
  295.8 8.2 %collective-permute-start = (f32[2,8,384]{2,1,0:T(8,128)S(1)}, f32[2,8,384]{2,1,0:T(8,128)S(1)}, u32[]{:S(2)}, u32[]{:S(2)}) collective-permute-start(f32[2,8,384]{2,1,0:T(8,128)S(1)} %get-tuple-element.315), channel_id=1, source_target_pairs={{0,1},{1,2},{2,3},{3,4},{4,5},{5,6},{6,7},{7,8},{8,9},{9,10},{10,1... | collective-permute-start | bytes 73736 | tf_op jit(solution)/shard_map/while/body/eval_jaxpr/ppermute | solution.py:15
  324.4 8.2 %collective-permute-start = (f32[2,8,384]{2,1,0:T(8,128)S(1)}, f32[2,8,384]{2,1,0:T(8,128)S(1)}, u32[]{:S(2)}, u32[]{:S(2)}) collective-permute-start(f32[2,8,384]{2,1,0:T(8,128)S(1)} %get-tuple-element.315), channel_id=1, source_target_pairs={{0,1},{1,2},{2,3},{3,4},{4,5},{5,6},{6,7},{7,8},{8,9},{9,10},{10,1... | collective-permute-start | bytes 73736 | tf_op jit(solution)/shard_map/while/body/eval_jaxpr/ppermute | solution.py:15
  353.0 8.2 %collective-permute-start = (f32[2,8,384]{2,1,0:T(8,128)S(1)}, f32[2,8,384]{2,1,0:T(8,128)S(1)}, u32[]{:S(2)}, u32[]{:S(2)}) collective-permute-start(f32[2,8,384]{2,1,0:T(8,128)S(1)} %get-tuple-element.315), channel_id=1, source_target_pairs={{0,1},{1,2},{2,3},{3,4},{4,5},{5,6},{6,7},{7,8},{8,9},{9,10},{10,1... | collective-permute-start | bytes 73736 | tf_op jit(solution)/shard_map/while/body/eval_jaxpr/ppermute | solution.py:15
  381.6 8.2 %collective-permute-start = (f32[2,8,384]{2,1,0:T(8,128)S(1)}, f32[2,8,384]{2,1,0:T(8,128)S(1)}, u32[]{:S(2)}, u32[]{:S(2)}) collective-permute-start(f32[2,8,384]{2,1,0:T(8,128)S(1)} %get-tuple-element.315), channel_id=1, source_target_pairs={{0,1},{1,2},{2,3},{3,4},{4,5},{5,6},{6,7},{7,8},{8,9},{9,10},{10,1... | collective-permute-start | bytes 73736 | tf_op jit(solution)/shard_map/while/body/eval_jaxpr/ppermute | solution.py:15
  410.2 8.2 %collective-permute-start = (f32[2,8,384]{2,1,0:T(8,128)S(1)}, f32[2,8,384]{2,1,0:T(8,128)S(1)}, u32[]{:S(2)}, u32[]{:S(2)}) collective-permute-start(f32[2,8,384]{2,1,0:T(8,128)S(1)} %get-tuple-element.315), channel_id=1, source_target_pairs={{0,1},{1,2},{2,3},{3,4},{4,5},{5,6},{6,7},{7,8},{8,9},{9,10},{10,1... | collective-permute-start | bytes 73736 | tf_op jit(solution)/shard_map/while/body/eval_jaxpr/ppermute | solution.py:15
  438.8 8.2 %collective-permute-start = (f32[2,8,384]{2,1,0:T(8,128)S(1)}, f32[2,8,384]{2,1,0:T(8,128)S(1)}, u32[]{:S(2)}, u32[]{:S(2)}) collective-permute-start(f32[2,8,384]{2,1,0:T(8,128)S(1)} %get-tuple-element.315), channel_id=1, source_target_pairs={{0,1},{1,2},{2,3},{3,4},{4,5},{5,6},{6,7},{7,8},{8,9},{9,10},{10,1... | collective-permute-start | bytes 73736 | tf_op jit(solution)/shard_map/while/body/eval_jaxpr/ppermute | solution.py:15
  467.4 8.2 %collective-permute-start = (f32[2,8,384]{2,1,0:T(8,128)S(1)}, f32[2,8,384]{2,1,0:T(8,128)S(1)}, u32[]{:S(2)}, u32[]{:S(2)}) collective-permute-start(f32[2,8,384]{2,1,0:T(8,128)S(1)} %get-tuple-element.315), channel_id=1, source_target_pairs={{0,1},{1,2},{2,3},{3,4},{4,5},{5,6},{6,7},{7,8},{8,9},{9,10},{10,1... | collective-permute-start | bytes 73736 | tf_op jit(solution)/shard_map/while/body/eval_jaxpr/ppermute | solution.py:15
  496.1 8.2 %collective-permute-start = (f32[2,8,384]{2,1,0:T(8,128)S(1)}, f32[2,8,384]{2,1,0:T(8,128)S(1)}, u32[]{:S(2)}, u32[]{:S(2)}) collective-permute-start(f32[2,8,384]{2,1,0:T(8,128)S(1)} %get-tuple-element.315), channel_id=1, source_target_pairs={{0,1},{1,2},{2,3},{3,4},{4,5},{5,6},{6,7},{7,8},{8,9},{9,10},{10,1... | collective-permute-start | bytes 73736 | tf_op jit(solution)/shard_map/while/body/eval_jaxpr/ppermute | solution.py:15
  (48 other events, 379.1 us)
where the time goes:
time: 536 us; the launch traced here: 528 us
  starting transfers between devices  210 us (39%)
  other arithmetic  155 us (29%)
  waiting for transfers between devices  90.4 us (17%)
  local copies, waits for them, and re-layouts  68.4 us (13%)
    mul x96, other arithmetic, update_block(): scale_w[:, level]  119 us
    ppermute x16, starting transfers between devices, shifted(): return lax.ppermute(block, axis, route)  112 us
    ppermute x18, starting transfers between devices, extended(): lax.ppermute(tail, axis, [(i, (i + 1) % count) for i in range(ends)])  53.8 us
    ppermute x18, waiting for transfers between devices, extended(): lax.ppermute(head, axis, [((i + 1) % count, i) for i in range(ends)])  47.4 us
    ppermute x18, starting transfers between devices, extended(): lax.ppermute(head, axis, [((i + 1) % count, i) for i in range(ends)])  44.1 us
    ppermute x18, waiting for transfers between devices, extended(): lax.ppermute(tail, axis, [(i, (i + 1) % count) for i in range(ends)])  24.6 us
    mul x16, other arithmetic, update_block(): slow_w[level] * previous  19.9 us
    ppermute x16, waiting for transfers between devices, shifted(): return lax.ppermute(block, axis, route)  18.4 us
  transfers between devices with their start and end apart: 52, of which 35 were waited for; matrix products, arithmetic and copies ran while one was open for 10% of the time, Pallas kernels for 0%

commit v1 on v0

v1 whole, which is shorter than its diff:
```python
import functools
import jax
import jax.numpy as jnp
from jax import lax
from jax.experimental import pallas as pl
from jax.experimental.pallas import tpu as pltpu
from jax.sharding import PartitionSpec as P

F32 = jnp.float32
VM = pltpu.VMEM
HALF = 8
DEEP = 16
COLS = 16
ROWS = 8 * DEEP + 8
AXES = ("sweep", "lat")


def whole(count):
    return [pl.BlockSpec(memory_space=VM)] * count


def place():
    s = lax.axis_index("sweep")
    return s // 2, s % 2


def split_kernel(tau, res, slow, att, near_ref, away_ref, sems):
    _, core = place()
    copies = []
    for k, (out, side) in enumerate(((away_ref, 1 - core), (near_ref, core))):
        for a, src in enumerate((tau.at[side], res.at[side], slow, att)):
            copies.append(pltpu.make_async_copy(src, out.at[a], sems.at[4 * k + a]))
    for copy in copies:
        copy.start()
    for copy in copies:
        copy.wait()


def pack_kernel(topo_ref, own_ref, got_ref, mid_ref, right_ref, left_ref):
    _, core = place()
    near, far = core * HALF, (1 - core) * HALF
    mid_ref[:, pl.ds(near, HALF)] = own_ref[...]
    mid_ref[:, pl.ds(far, HALF)] = got_ref[...]
    row = lax.broadcasted_iota(jnp.int32, (COLS, topo_ref.shape[1]), 0)
    for a in range(4):
        base = a * ROWS
        right_ref[base : base + COLS] = mid_ref[a, 0]
        left_ref[base : base + COLS] = mid_ref[a, 0]
        for j in range(1, 8):
            at = base + COLS * j
            near_plane, far_plane = mid_ref[a, j], mid_ref[a, DEEP - j]
            right_ref[at : at + COLS] = jnp.where(row >= j, near_plane, pltpu.roll(far_plane, j, 0))
            left_ref[at : at + COLS] = jnp.where(row < COLS - j, near_plane, pltpu.roll(far_plane, COLS - j, 0))
        at = base + COLS * 8
        right_ref[at : at + 8] = mid_ref[a, 8, 8:16]
        left_ref[at : at + 8] = mid_ref[a, 8, 0:8]
    topo = topo_ref[...].astype(F32)
    right_ref[4 * ROWS : 4 * ROWS + COLS] = topo
    left_ref[4 * ROWS : 4 * ROWS + COLS] = topo


def band(j):
    halo = 15 - j
    trim = 0 if halo > 8 else 8 if halo > 0 else 16
    return trim, 3 * COLS - trim


def coef_kernel(mid_ref, west_ref, east_ref, topo_ref, src_o, mid_o, west_o, east_o, north_o, south_o):
    depth, lat, lats = place()[0] * DEEP, lax.axis_index("lat"), lax.axis_size("lat")
    rows = topo_ref.shape[1]
    wide = (3 * COLS, rows)
    col = lax.broadcasted_iota(jnp.int32, wide, 0)
    cross = lax.broadcasted_iota(jnp.int32, wide, 1)
    first, last = cross == 0, cross == rows - 1
    inside = ((col >= COLS) | (lat > 0)) & ((col < 2 * COLS) | (lat < lats - 1))
    top = 4 * ROWS
    topo = jnp.concatenate([west_ref[top : top + COLS], topo_ref[...].astype(F32), east_ref[top : top + COLS]], axis=0)
    topo = jnp.where(inside, topo, 1e6)

    def window(a, j):
        base = a * ROWS
        if j <= 7:
            at = base + COLS * j
            west, east = west_ref[at : at + COLS], east_ref[at : at + COLS]
        elif j == 8:
            at = base + COLS * 8
            west, east = west_ref[at : at + 8], east_ref[at : at + 8]
            west, east = jnp.concatenate([west, west], axis=0), jnp.concatenate([east, east], axis=0)
        else:
            at = base + COLS * (DEEP - j)
            west = pltpu.roll(west_ref[at : at + COLS], j, 0)
            east = pltpu.roll(east_ref[at : at + COLS], DEEP - j, 0)
        return jnp.concatenate([west, mid_ref[a, j], east], axis=0)

    for j in range(DEEP):
        lo, hi = (0, 3 * COLS) if j < HALF else (8, 3 * COLS - 8)
        count = hi - lo
        tau = window(0, j)[lo:hi]
        slow = window(2, j)[lo:hi]
        active = (topo[lo:hi] <= (depth + j).astype(F32)).astype(F32)
        step_x = tau - pltpu.roll(tau, 1, 0)
        before = jnp.where(first[lo:hi], 0.0, pltpu.roll(tau, 1, 1))
        step_y = tau - before
        flat_x = jnp.log(1.0 + jnp.exp(-jnp.abs(step_x)))
        flat_y = jnp.log(1.0 + jnp.exp(-jnp.abs(step_y)))
        edge = tau[:, rows - 128 :]
        edge = jnp.maximum(edge, 0.0) + jnp.log(1.0 + jnp.exp(-jnp.abs(edge)))
        west = jnp.maximum(step_x, 0.0) + flat_x
        east = pltpu.roll(jnp.maximum(-step_x, 0.0) + flat_x, count - 1, 0)
        north = jnp.maximum(step_y, 0.0) + flat_y
        south = pltpu.roll(jnp.maximum(-step_y, 0.0) + flat_y, rows - 1, 1)
        edge = jnp.where(last[lo:hi, rows - 128 :], edge, south[:, rows - 128 :])
        south = jnp.concatenate([south[:, : rows - 128], edge], axis=1)
        scale = active / (slow + west + east + north + south + window(3, j)[lo:hi])
        src_o[j, lo:hi] = scale * window(1, j)[lo:hi]
        mid_o[j, lo:hi] = scale * slow
        west_o[j, lo:hi] = scale * west
        east_o[j, lo:hi] = scale * east
        north_o[j, lo:hi] = jnp.where(first[lo:hi], 0.0, scale * north)
        south_o[j, lo:hi] = jnp.where(last[lo:hi], 0.0, scale * south)


def sweep_kernel(turn, *refs):
    src, mid, west, east, north, south = refs[:6]
    keep_ref, give_ref, end_ref, buf_ref, sems = refs[-5:]
    stage, core = place()

    @pl.when(stage == turn)
    def _():
        rows = src.shape[2]
        if turn:
            level = jnp.concatenate([r[...] for r in refs[6:9]], axis=0)
        at = 0
        for j in range(DEEP):
            lo, hi = band(j)
            if turn == 0 and j == 0:
                level = src[j, lo:hi]
            else:
                count = level.shape[0]
                down, up = pltpu.roll(level, 1, 0), pltpu.roll(level, count - 1, 0)
                before, after = pltpu.roll(level, 1, 1), pltpu.roll(level, rows - 1, 1)
                cut = lo - at
                if cut:
                    level, down, up, before, after = (v[cut : count - cut] for v in (level, down, up, before, after))
                level = (
                    src[j, lo:hi]
                    + mid[j, lo:hi] * level
                    + west[j, lo:hi] * down
                    + east[j, lo:hi] * up
                    + north[j, lo:hi] * before
                    + south[j, lo:hi] * after
                )
            at = lo
            buf_ref[j] = level[COLS - lo : 2 * COLS - lo]
        end_ref[...] = level[COLS - at : 2 * COLS - at]
        kept = pltpu.make_async_copy(buf_ref.at[pl.ds(core * HALF, HALF)], keep_ref, sems.at[0])
        gave = pltpu.make_async_copy(buf_ref.at[pl.ds((1 - core) * HALF, HALF)], give_ref, sems.at[1])
        kept.start()
        gave.start()
        kept.wait()
        gave.wait()


def finish_kernel(kept_ref, got_ref, slow_ref, adjoint_ref, gradient_ref):
    _, core = place()
    own, got = kept_ref[...], got_ref[...]
    adjoint_ref[core] = own
    adjoint_ref[1 - core] = got
    gradient_ref[...] = slow_ref[...] * (own + got)


def shards(traveltime, residual, slowness, attenuation, topography):
    columns, crosses = topography.shape
    sweeps, lats = lax.axis_size("sweep"), lax.axis_size("lat")
    stages = sweeps // 2
    hbm = pl.BlockSpec(memory_space=pltpu.HBM)
    block = (HALF, columns, crosses)

    def shape(*dims):
        return jax.ShapeDtypeStruct(dims, F32)

    def call(kernel, outs, ins, vmem=4 << 20, in_specs=None, out_specs=None, **kw):
        return pl.pallas_call(
            kernel,
            out_shape=outs,
            in_specs=in_specs or whole(len(ins)),
            out_specs=out_specs or whole(len(outs)),
            compiler_params=pltpu.CompilerParams(vmem_limit_bytes=vmem),
            **kw,
        )(*ins)

    swap = [(i, i ^ 1) for i in range(sweeps)]
    near, away = call(
        split_kernel,
        (shape(4, *block),) * 2,
        (traveltime, residual, slowness, attenuation),
        vmem=60 << 20,
        in_specs=[hbm] * 4,
        scratch_shapes=[pltpu.SemaphoreType.DMA((8,))],
    )
    got = lax.ppermute(away, "sweep", swap)
    packed = shape(4 * ROWS + columns, crosses)
    centre, to_right, to_left = call(
        pack_kernel, (shape(4, DEEP, columns, crosses), packed, packed), (topography, near, got)
    )
    from_west = lax.ppermute(to_right, "lat", [(i, i + 1) for i in range(lats - 1)])
    from_east = lax.ppermute(to_left, "lat", [(i + 1, i) for i in range(lats - 1)])
    coefs = call(
        coef_kernel,
        (shape(DEEP, 3 * columns, crosses),) * 6,
        (centre, from_west, from_east, topography),
        vmem=16 << 20,
    )

    def hop(value, turn, side):
        pairs = []
        for i in (2 * turn, 2 * turn + 1):
            for k in range(lats):
                if 0 <= k + side < lats:
                    pairs.append((i * lats + k, (i + 2) * lats + k + side))
        return lax.ppermute(value, AXES, pairs)

    near_end = ()
    for turn in range(stages):
        ins = (*coefs, *near_end)
        keep, give, end = call(
            functools.partial(sweep_kernel, turn),
            (shape(*block), shape(*block), shape(columns, crosses)),
            ins,
            in_specs=whole(len(ins) - (2 if turn else 0)) + [hbm] * (2 if turn else 0),
            out_specs=[hbm, hbm] + whole(1),
            input_output_aliases={9: 0, 10: 1} if turn else {},
            scratch_shapes=[VM((DEEP, columns, crosses), F32), pltpu.SemaphoreType.DMA((2,))],
        )
        if turn < stages - 1:
            low, high, own = hop(end, turn, 1), hop(end, turn, -1), hop(end, turn, 0)
            near_end = (low, own, high, keep, give)
    given = lax.ppermute(give, "sweep", swap)
    return call(finish_kernel, (shape(2, *block), shape(*block)), (keep, given, slowness))


def solution(mesh):
    in_specs = (
        P(None, "sweep", "lat", None),
        P(None, "sweep", "lat", None),
        P("sweep", "lat", None),
        P("sweep", "lat", None),
        P("lat", None),
    )
    out_specs = (P(None, "sweep", "lat", None), P("sweep", "lat", None))
    return jax.shard_map(shards, mesh=mesh, in_specs=in_specs, out_specs=out_specs, check_vma=False)
```

time: 536 us -> 110 us (0.21)
  the two profiles are of different devices: /device:TPU:223 before, /device:TPU:481 now
where the time goes in v1:
time: 110 us
  waiting for transfers between devices  62.1 us (56%)
  starting transfers between devices  36.8 us (33%)
  Pallas kernels  8.6 us (8%)
  local copies, waits for them, and re-layouts  1.14 us (1%)
    ppermute x21, waiting for transfers between devices, hop(): return lax.ppermute(value, AXES, pairs)  41.1 us
    ppermute x1, waiting for transfers between devices, shards(): lax.ppermute(to_right, 'lat', [(i, i + 1) for i in range(lats - 1)])  16.9 us
    ppermute x21, starting transfers between devices, hop(): return lax.ppermute(value, AXES, pairs)  15.8 us
    ppermute x1, starting transfers between devices, shards(): given = lax.ppermute(give, 'sweep', swap)  9.77 us
    pallas_call x12, Pallas kernels, call(): pl.pallas_call(kernel, out_shape=outs, in_specs=in_specs or whole(len(ins...  8.6 us
    ppermute x1, starting transfers between devices, shards(): lax.ppermute(to_left, 'lat', [(i + 1, i) for i in range(lats - 1)])  5.48 us
    ppermute x1, starting transfers between devices, shards(): lax.ppermute(to_right, 'lat', [(i, i + 1) for i in range(lats - 1)])  3.12 us
    ppermute x1, starting transfers between devices, shards(): got = lax.ppermute(away, 'sweep', swap)  2.58 us
  transfers between devices with their start and end apart: 25, of which 7 were waited for; matrix products, arithmetic and copies ran while one was open for 0% of the time, Pallas kernels for 0%

profile of v1, /device:TPU:481, one launch (start us, length us, event | category | flops | bytes accessed | tf_op | source)
XLA Modules:
  0.0 109.7 jit_solution(6888481752559301649)
XLA Ops:
  0.6 2.7 %shard_map.68 = (f32[4,8,16,384]{3,2,1,0:T(8,128)}, f32[4,8,16,384]{3,2,1,0:T(8,128)}) custom-call(f32[2,8,16,384]{3,2,1,0:T(8,128)} %tau.1, f32[2,8,16,384]{3,2,1,0:T(8,128)} %res.1, f32[8,16,384]{2,1,0:T(8,128)} %slow_ref.1, f32[8,16,384]{2,1,0:T(8,128)} %att.1), custom_call_target="tpu_custom_call" | custom-call | tf_op jit(solution)/shard_map/pallas_call | solution.py:183
  3.4 2.6 %collective-permute-start = (f32[4,8,16,384]{3,2,1,0:T(8,128)}, f32[4,8,16,384]{3,2,1,0:T(8,128)S(1)}, u32[]{:S(2)}, u32[]{:S(2)}) collective-permute-start(f32[4,8,16,384]{3,2,1,0:T(8,128)} %get-tuple-element.37), channel_id=1, source_target_pairs={{0,32},{32,0},{64,96},{96,64},{128,160},{160,128},{192,224},{224,1... | collective-permute-start | bytes 2359304 | tf_op jit(solution)/shard_map/ppermute | solution.py:201
  6.0 2.1 %collective-permute-done.got_ref = f32[4,8,16,384]{3,2,1,0:T(8,128)S(1)} collective-permute-done((f32[4,8,16,384]{3,2,1,0:T(8,128)}, f32[4,8,16,384]{3,2,1,0:T(8,128)S(1)}, u32[]{:S(2)}, u32[]{:S(2)}) %collective-permute-start) | collective-permute-done | bytes 786464 | tf_op jit(solution)/shard_map/ppermute | solution.py:201
  8.1 1.1 %copy-done = f32[4,8,16,384]{3,2,1,0:T(8,128)S(1)} copy-done((f32[4,8,16,384]{3,2,1,0:T(8,128)S(1)}, f32[4,8,16,384]{3,2,1,0:T(8,128)}, u32[]{:S(2)}) %copy-start) | copy-done | bytes 786456
  9.5 3.1 %collective-permute-start.1 = (f32[560,384]{1,0:T(8,128)S(1)}, f32[560,384]{1,0:T(8,128)S(1)}, u32[]{:S(2)}, u32[]{:S(2)}) collective-permute-start(f32[560,384]{1,0:T(8,128)S(1)} %get-tuple-element.39), channel_id=1, source_target_pairs={{0,1},{1,2},{2,3},{3,4},{4,5},{5,6},{6,7},{7,8},{8,9},{9,10},{10,1... | collective-permute-start | bytes 2580488 | tf_op jit(solution)/shard_map/ppermute | solution.py:206
  12.6 5.5 %collective-permute-start.2 = (f32[560,384]{1,0:T(8,128)S(1)}, f32[560,384]{1,0:T(8,128)S(1)}, u32[]{:S(2)}, u32[]{:S(2)}) collective-permute-start(f32[560,384]{1,0:T(8,128)S(1)} %get-tuple-element.40), channel_id=1, source_target_pairs={{1,0},{2,1},{3,2},{4,3},{5,4},{6,5},{7,6},{8,7},{9,8},{10,9},{11,1... | collective-permute-start | bytes 2580488 | tf_op jit(solution)/shard_map/ppermute | solution.py:207
  18.1 16.9 %collective-permute-done.1.west_ref = f32[560,384]{1,0:T(8,128)S(1)} collective-permute-done((f32[560,384]{1,0:T(8,128)S(1)}, f32[560,384]{1,0:T(8,128)S(1)}, u32[]{:S(2)}, u32[]{:S(2)}) %collective-permute-start.1) | collective-permute-done | bytes 860192 | tf_op jit(solution)/shard_map/ppermute | solution.py:206
  35.0 0.9 collective-permute-done.2.east_ref
  35.9 2.1 %shard_map.70 = (f32[16,48,384]{2,1,0:T(8,128)S(1)}, f32[16,48,384]{2,1,0:T(8,128)S(1)}, f32[16,48,384]{2,1,0:T(8,128)S(1)}, f32[16,48,384]{2,1,0:T(8,128)S(1)},...) custom-call(f32[4,16,16,384]{3,2,1,0:T(8,128)S(1)} %get-tuple-element.38.mid_ref, ...), custom_call_target="tpu_custom_call" | custom-call | tf_op jit(solution)/shard_map/pallas_call | solution.py:183
  38.0 0.7 collective-permute-start.5
  38.7 0.7 collective-permute-start.4
  41.4 0.7 collective-permute-start.6
  42.2 0.7 collective-permute-start.11
  42.9 0.7 collective-permute-start.10
  50.6 1.3 %collective-permute-start.23 = (f32[16,384]{1,0:T(8,128)S(1)}, f32[16,384]{1,0:T(8,128)S(1)}, u32[]{:S(2)}, u32[]{:S(2)}) collective-permute-start(f32[16,384]{1,0:T(8,128)S(1)} %get-tuple-element.65), channel_id=1, source_target_pairs={{385,448},{386,449},{387,450},{388,451},{389,452},{390,453},{391,4... | collective-permute-start | bytes 73736 | tf_op jit(solution)/shard_map/ppermute | solution.py:221
  51.9 1.3 %collective-permute-start.22 = (f32[16,384]{1,0:T(8,128)S(1)}, f32[16,384]{1,0:T(8,128)S(1)}, u32[]{:S(2)}, u32[]{:S(2)}) collective-permute-start(f32[16,384]{1,0:T(8,128)S(1)} %get-tuple-element.65), channel_id=1, source_target_pairs={{384,448},{385,449},{386,450},{387,451},{388,452},{389,453},{390,4... | collective-permute-start | bytes 73736 | tf_op jit(solution)/shard_map/ppermute | solution.py:221
  53.2 1.3 %collective-permute-start.21 = (f32[16,384]{1,0:T(8,128)S(1)}, f32[16,384]{1,0:T(8,128)S(1)}, u32[]{:S(2)}, u32[]{:S(2)}) collective-permute-start(f32[16,384]{1,0:T(8,128)S(1)} %get-tuple-element.65), channel_id=1, source_target_pairs={{384,449},{385,450},{386,451},{387,452},{388,453},{389,454},{390,4... | collective-permute-start | bytes 73736 | tf_op jit(solution)/shard_map/ppermute | solution.py:221
  54.5 37.8 %collective-permute-done.23.refs_8_ = f32[16,384]{1,0:T(8,128)S(1)} collective-permute-done((f32[16,384]{1,0:T(8,128)S(1)}, f32[16,384]{1,0:T(8,128)S(1)}, u32[]{:S(2)}, u32[]{:S(2)}) %collective-permute-start.23) | collective-permute-done | bytes 24608 | tf_op jit(solution)/shard_map/ppermute | solution.py:221
  92.2 2.1 %collective-permute-done.22.refs_7_ = f32[16,384]{1,0:T(8,128)S(1)} collective-permute-done((f32[16,384]{1,0:T(8,128)S(1)}, f32[16,384]{1,0:T(8,128)S(1)}, u32[]{:S(2)}, u32[]{:S(2)}) %collective-permute-start.22) | collective-permute-done | bytes 24608 | tf_op jit(solution)/shard_map/ppermute | solution.py:221
  94.3 1.2 %collective-permute-done.21.refs_6_ = f32[16,384]{1,0:T(8,128)S(1)} collective-permute-done((f32[16,384]{1,0:T(8,128)S(1)}, f32[16,384]{1,0:T(8,128)S(1)}, u32[]{:S(2)}, u32[]{:S(2)}) %collective-permute-start.21) | collective-permute-done | bytes 24608 | tf_op jit(solution)/shard_map/ppermute | solution.py:221
  95.6 2.4 %shard_map.78 = (f32[8,16,384]{2,1,0:T(8,128)S(1)}, f32[8,16,384]{2,1,0:T(8,128)S(1)}, f32[16,384]{1,0:T(8,128)}) custom-call(f32[16,48,384]{2,1,0:T(8,128)S(1)} %get-tuple-element.41.refs_0_, f32[16,48,384]{2,1,0:T(8,128)S(1)} %get-tuple-element.42.refs_1_, ...), custom_call_target="tpu_custom_call", output_to_operand_aliasing={{0}: (9, {}), {1}: (10, {})} | custom-call | tf_op jit(solution)/shard_map/pallas_call | solution.py:183
  98.0 9.8 %collective-permute-start.24 = (f32[8,16,384]{2,1,0:T(8,128)S(1)}, f32[8,16,384]{2,1,0:T(8,128)S(1)}, u32[]{:S(2)}, u32[]{:S(2)}) collective-permute-start(f32[8,16,384]{2,1,0:T(8,128)S(1)} %get-tuple-element.69), channel_id=1, source_target_pairs={{0,32},{32,0},{64,96},{96,64},{128,160},{160,128},{192,224},{224,1... | collective-permute-start | bytes 589832 | tf_op jit(solution)/shard_map/ppermute | solution.py:238
  107.7 1.0 collective-permute-done.24.got_ref
  108.8 0.9 shard_map.79
  (44 shorter events, 9.2 us)
Async XLA Ops:
  3.4 4.7 %collective-permute-start = (f32[4,8,16,384]{3,2,1,0:T(8,128)}, f32[4,8,16,384]{3,2,1,0:T(8,128)S(1)}, u32[]{:S(2)}, u32[]{:S(2)}) collective-permute-start(f32[4,8,16,384]{3,2,1,0:T(8,128)} %get-tuple-element.37), channel_id=1, source_target_pairs={{0,32},{32,0},{64,96},{96,64},{128,160},{160,128},{192,224},{224,1... | collective-permute-start | bytes 2359304 | tf_op jit(solution)/shard_map/ppermute | solution.py:201
  9.5 25.5 %collective-permute-start.1 = (f32[560,384]{1,0:T(8,128)S(1)}, f32[560,384]{1,0:T(8,128)S(1)}, u32[]{:S(2)}, u32[]{:S(2)}) collective-permute-start(f32[560,384]{1,0:T(8,128)S(1)} %get-tuple-element.39), channel_id=1, source_target_pairs={{0,1},{1,2},{2,3},{3,4},{4,5},{5,6},{6,7},{7,8},{8,9},{9,10},{10,1... | collective-permute-start | bytes 2580488 | tf_op jit(solution)/shard_map/ppermute | solution.py:206
  12.6 23.3 %collective-permute-start.2 = (f32[560,384]{1,0:T(8,128)S(1)}, f32[560,384]{1,0:T(8,128)S(1)}, u32[]{:S(2)}, u32[]{:S(2)}) collective-permute-start(f32[560,384]{1,0:T(8,128)S(1)} %get-tuple-element.40), channel_id=1, source_target_pairs={{1,0},{2,1},{3,2},{4,3},{5,4},{6,5},{7,6},{8,7},{9,8},{10,9},{11,1... | collective-permute-start | bytes 2580488 | tf_op jit(solution)/shard_map/ppermute | solution.py:207
  38.0 2.0 %collective-permute-start.5 = (f32[16,384]{1,0:T(8,128)S(1)}, f32[16,384]{1,0:T(8,128)S(1)}, u32[]{:S(2)}, u32[]{:S(2)}) collective-permute-start(f32[16,384]{1,0:T(8,128)S(1)} %get-tuple-element.47), channel_id=1, source_target_pairs={{1,64},{2,65},{3,66},{4,67},{5,68},{6,69},{7,70},{8,71},{9,72},{10... | collective-permute-start | bytes 73736 | tf_op jit(solution)/shard_map/ppermute | solution.py:221
  38.7 1.4 %collective-permute-start.4 = (f32[16,384]{1,0:T(8,128)S(1)}, f32[16,384]{1,0:T(8,128)S(1)}, u32[]{:S(2)}, u32[]{:S(2)}) collective-permute-start(f32[16,384]{1,0:T(8,128)S(1)} %get-tuple-element.47), channel_id=1, source_target_pairs={{0,64},{1,65},{2,66},{3,67},{4,68},{5,69},{6,70},{7,71},{8,72},{9,... | collective-permute-start | bytes 73736 | tf_op jit(solution)/shard_map/ppermute | solution.py:221
  39.3 0.7 collective-permute-start.3
  40.1 2.0 %collective-permute-start.8 = (f32[16,384]{1,0:T(8,128)S(1)}, f32[16,384]{1,0:T(8,128)S(1)}, u32[]{:S(2)}, u32[]{:S(2)}) collective-permute-start(f32[16,384]{1,0:T(8,128)S(1)} %get-tuple-element.50), channel_id=1, source_target_pairs={{65,128},{66,129},{67,130},{68,131},{69,132},{70,133},{71,134},{72... | collective-permute-start | bytes 73736 | tf_op jit(solution)/shard_map/ppermute | solution.py:221
  40.8 1.4 %collective-permute-start.7 = (f32[16,384]{1,0:T(8,128)S(1)}, f32[16,384]{1,0:T(8,128)S(1)}, u32[]{:S(2)}, u32[]{:S(2)}) collective-permute-start(f32[16,384]{1,0:T(8,128)S(1)} %get-tuple-element.50), channel_id=1, source_target_pairs={{64,128},{65,129},{66,130},{67,131},{68,132},{69,133},{70,134},{71... | collective-permute-start | bytes 73736 | tf_op jit(solution)/shard_map/ppermute | solution.py:221
  41.4 0.7 collective-permute-start.6
  42.2 2.0 %collective-permute-start.11 = (f32[16,384]{1,0:T(8,128)S(1)}, f32[16,384]{1,0:T(8,128)S(1)}, u32[]{:S(2)}, u32[]{:S(2)}) collective-permute-start(f32[16,384]{1,0:T(8,128)S(1)} %get-tuple-element.53), channel_id=1, source_target_pairs={{129,192},{130,193},{131,194},{132,195},{133,196},{134,197},{135,1... | collective-permute-start | bytes 73736 | tf_op jit(solution)/shard_map/ppermute | solution.py:221
  42.9 1.4 %collective-permute-start.10 = (f32[16,384]{1,0:T(8,128)S(1)}, f32[16,384]{1,0:T(8,128)S(1)}, u32[]{:S(2)}, u32[]{:S(2)}) collective-permute-start(f32[16,384]{1,0:T(8,128)S(1)} %get-tuple-element.53), channel_id=1, source_target_pairs={{128,192},{129,193},{130,194},{131,195},{132,196},{133,197},{134,1... | collective-permute-start | bytes 73736 | tf_op jit(solution)/shard_map/ppermute | solution.py:221
  43.5 0.7 collective-permute-start.9
  44.3 2.0 %collective-permute-start.14 = (f32[16,384]{1,0:T(8,128)S(1)}, f32[16,384]{1,0:T(8,128)S(1)}, u32[]{:S(2)}, u32[]{:S(2)}) collective-permute-start(f32[16,384]{1,0:T(8,128)S(1)} %get-tuple-element.56), channel_id=1, source_target_pairs={{193,256},{194,257},{195,258},{196,259},{197,260},{198,261},{199,2... | collective-permute-start | bytes 73736 | tf_op jit(solution)/shard_map/ppermute | solution.py:221
  45.0 1.4 %collective-permute-start.13 = (f32[16,384]{1,0:T(8,128)S(1)}, f32[16,384]{1,0:T(8,128)S(1)}, u32[]{:S(2)}, u32[]{:S(2)}) collective-permute-start(f32[16,384]{1,0:T(8,128)S(1)} %get-tuple-element.56), channel_id=1, source_target_pairs={{192,256},{193,257},{194,258},{195,259},{196,260},{197,261},{198,2... | collective-permute-start | bytes 73736 | tf_op jit(solution)/shard_map/ppermute | solution.py:221
  45.6 0.7 collective-permute-start.12
  46.4 2.0 %collective-permute-start.17 = (f32[16,384]{1,0:T(8,128)S(1)}, f32[16,384]{1,0:T(8,128)S(1)}, u32[]{:S(2)}, u32[]{:S(2)}) collective-permute-start(f32[16,384]{1,0:T(8,128)S(1)} %get-tuple-element.59), channel_id=1, source_target_pairs={{257,320},{258,321},{259,322},{260,323},{261,324},{262,325},{263,3... | collective-permute-start | bytes 73736 | tf_op jit(solution)/shard_map/ppermute | solution.py:221
  47.0 1.4 %collective-permute-start.16 = (f32[16,384]{1,0:T(8,128)S(1)}, f32[16,384]{1,0:T(8,128)S(1)}, u32[]{:S(2)}, u32[]{:S(2)}) collective-permute-start(f32[16,384]{1,0:T(8,128)S(1)} %get-tuple-element.59), channel_id=1, source_target_pairs={{256,320},{257,321},{258,322},{259,323},{260,324},{261,325},{262,3... | collective-permute-start | bytes 73736 | tf_op jit(solution)/shard_map/ppermute | solution.py:221
  48.5 2.0 %collective-permute-start.20 = (f32[16,384]{1,0:T(8,128)S(1)}, f32[16,384]{1,0:T(8,128)S(1)}, u32[]{:S(2)}, u32[]{:S(2)}) collective-permute-start(f32[16,384]{1,0:T(8,128)S(1)} %get-tuple-element.62), channel_id=1, source_target_pairs={{321,384},{322,385},{323,386},{324,387},{325,388},{326,389},{327,3... | collective-permute-start | bytes 73736 | tf_op jit(solution)/shard_map/ppermute | solution.py:221
  49.1 1.4 %collective-permute-start.19 = (f32[16,384]{1,0:T(8,128)S(1)}, f32[16,384]{1,0:T(8,128)S(1)}, u32[]{:S(2)}, u32[]{:S(2)}) collective-permute-start(f32[16,384]{1,0:T(8,128)S(1)} %get-tuple-element.62), channel_id=1, source_target_pairs={{320,384},{321,385},{322,386},{323,387},{324,388},{325,389},{326,3... | collective-permute-start | bytes 73736 | tf_op jit(solution)/shard_map/ppermute | solution.py:221
  49.8 0.7 collective-permute-start.18
  50.6 41.7 %collective-permute-start.23 = (f32[16,384]{1,0:T(8,128)S(1)}, f32[16,384]{1,0:T(8,128)S(1)}, u32[]{:S(2)}, u32[]{:S(2)}) collective-permute-start(f32[16,384]{1,0:T(8,128)S(1)} %get-tuple-element.65), channel_id=1, source_target_pairs={{385,448},{386,449},{387,450},{388,451},{389,452},{390,453},{391,4... | collective-permute-start | bytes 73736 | tf_op jit(solution)/shard_map/ppermute | solution.py:221
  51.9 42.5 %collective-permute-start.22 = (f32[16,384]{1,0:T(8,128)S(1)}, f32[16,384]{1,0:T(8,128)S(1)}, u32[]{:S(2)}, u32[]{:S(2)}) collective-permute-start(f32[16,384]{1,0:T(8,128)S(1)} %get-tuple-element.65), channel_id=1, source_target_pairs={{384,448},{385,449},{386,450},{387,451},{388,452},{389,453},{390,4... | collective-permute-start | bytes 73736 | tf_op jit(solution)/shard_map/ppermute | solution.py:221
  53.2 42.4 %collective-permute-start.21 = (f32[16,384]{1,0:T(8,128)S(1)}, f32[16,384]{1,0:T(8,128)S(1)}, u32[]{:S(2)}, u32[]{:S(2)}) collective-permute-start(f32[16,384]{1,0:T(8,128)S(1)} %get-tuple-element.65), channel_id=1, source_target_pairs={{384,449},{385,450},{386,451},{387,452},{388,453},{389,454},{390,4... | collective-permute-start | bytes 73736 | tf_op jit(solution)/shard_map/ppermute | solution.py:221
  98.0 10.8 %collective-permute-start.24 = (f32[8,16,384]{2,1,0:T(8,128)S(1)}, f32[8,16,384]{2,1,0:T(8,128)S(1)}, u32[]{:S(2)}, u32[]{:S(2)}) collective-permute-start(f32[8,16,384]{2,1,0:T(8,128)S(1)} %get-tuple-element.69), channel_id=1, source_target_pairs={{0,32},{32,0},{64,96},{96,64},{128,160},{160,128},{192,224},{224,1... | collective-permute-start | bytes 589832 | tf_op jit(solution)/shard_map/ppermute | solution.py:238
  (4 other events, 22.5 us)

commit v2 on v1

v2 whole, which is shorter than its diff:
```python
import functools
import jax
import jax.numpy as jnp
from jax import lax
from jax.experimental import pallas as pl
from jax.experimental.pallas import tpu as pltpu
from jax.sharding import PartitionSpec as P

F32 = jnp.float32
VM = pltpu.VMEM
HALF = 8
DEEP = 16
COLS = 16
SIDE = 8
EDGE = 5 * SIDE
SKIRT = HALF * SIDE
AXES = ("sweep", "lat")


def whole(count):
    return [pl.BlockSpec(memory_space=VM)] * count


def place():
    s = lax.axis_index("sweep")
    return s // 2, s % 2


def split_kernel(tau, res, slow, att, near_ref, away_ref, sems):
    _, core = place()
    copies = []
    for k, (out, side) in enumerate(((away_ref, 1 - core), (near_ref, core))):
        for a, src in enumerate((tau.at[side], res.at[side], slow, att)):
            copies.append(pltpu.make_async_copy(src, out.at[a], sems.at[4 * k + a]))
    for copy in copies:
        copy.start()
    for copy in copies:
        copy.wait()


def land_kernel(near_hbm, near_ref, sem):
    copy = pltpu.make_async_copy(near_hbm, near_ref, sem)
    copy.start()
    copy.wait()


def pack_edges(mid_ref, base, right_ref, left_ref, row):
    for a in range(4):
        for i in range(5):
            at = a * EDGE + SIDE * i
            right, left = mid_ref[a, base + i, SIDE:COLS], mid_ref[a, base + i, :SIDE]
            if 0 < i < 4:
                far = HALF - i
                right = jnp.where(row >= i, right, pltpu.roll(mid_ref[a, base + far, SIDE:COLS], i, 0))
                left = jnp.where(row < far, left, pltpu.roll(mid_ref[a, base + far, :SIDE], far, 0))
            right_ref[at : at + SIDE] = right
            left_ref[at : at + SIDE] = left


def pack_kernel(topo_ref, near_ref, got_ref, mid_ref, a_right, a_left, b_right, b_left):
    _, core = place()
    mid_ref[:, pl.ds(core * HALF, HALF)] = near_ref[...]
    mid_ref[:, pl.ds((1 - core) * HALF, HALF)] = got_ref[...]
    row = lax.broadcasted_iota(jnp.int32, (SIDE, topo_ref.shape[1]), 0)
    pack_edges(mid_ref, 0, a_right, a_left, row)
    pack_edges(mid_ref, HALF, b_right, b_left, row)
    topo = topo_ref[...].astype(F32)
    for right, left in ((a_right, a_left), (b_right, b_left)):
        right[4 * EDGE :] = topo[SIDE:]
        left[4 * EDGE :] = topo[:SIDE]


def skirt_kernel(mid_ref, topo_ref, right_ref, left_ref):
    row = lax.broadcasted_iota(jnp.int32, (SIDE, topo_ref.shape[1]), 0)
    for a in range(4):
        for i in range(HALF):
            at = a * SKIRT + SIDE * i
            low, high = mid_ref[a, i, :SIDE], mid_ref[a, i, SIDE:COLS]
            right_ref[at : at + SIDE] = jnp.where(row >= i, low, high)
            left_ref[at : at + SIDE] = jnp.where(row < HALF - i, high, low)
    topo = topo_ref[...].astype(F32)
    right_ref[4 * SKIRT :] = topo[:SIDE]
    left_ref[4 * SKIRT :] = topo[SIDE:]


def edge_tiles(west_ref, east_ref, a, i):
    if i <= 4:
        at = a * EDGE + SIDE * i
        return west_ref[at : at + SIDE], east_ref[at : at + SIDE]
    k = HALF - i
    at = a * EDGE + SIDE * k
    return pltpu.roll(west_ref[at : at + SIDE], SIDE - k, 0), pltpu.roll(east_ref[at : at + SIDE], k, 0)


def coef_kernel(base, mid_ref, topo_ref, west_ref, east_ref, *refs):
    outs, skirts = refs[-6:], refs[:-6]
    src_o, mid_o, west_o, east_o, north_o, south_o = outs
    count, rows = src_o.shape[1:]
    halo = (count - COLS) // 2
    stage, _ = place()
    lat, lats = lax.axis_index("lat"), lax.axis_size("lat")
    depth = stage * DEEP + base
    col = lax.broadcasted_iota(jnp.int32, (count, rows), 0)
    cross = lax.broadcasted_iota(jnp.int32, (count, rows), 1)
    row = lax.broadcasted_iota(jnp.int32, (SIDE, rows), 0)
    first, last = cross == 0, cross == rows - 1
    inside = ((col >= halo) | (lat > 0)) & ((col < halo + COLS) | (lat < lats - 1))
    topo = [west_ref[4 * EDGE :], topo_ref[...].astype(F32), east_ref[4 * EDGE :]]
    if skirts:
        topo = [skirts[0][4 * SKIRT :]] + topo + [skirts[1][4 * SKIRT :]]
    topo = jnp.where(inside, jnp.concatenate(topo, axis=0), 1e6)

    def window(a, i):
        west, east = edge_tiles(west_ref, east_ref, a, i)
        tiles = [west, mid_ref[a, base + i], east]
        if skirts:
            at = a * SKIRT + SIDE * i
            far_west, far_east = skirts[0][at : at + SIDE], skirts[1][at : at + SIDE]
            tiles[0] = jnp.where(row >= i, west, far_west)
            tiles[2] = jnp.where(row < HALF - i, east, far_east)
            tiles = [far_west] + tiles + [far_east]
        return jnp.concatenate(tiles, axis=0)

    for i in range(HALF):
        tau = window(0, i)
        slow = window(2, i)
        active = (topo <= (depth + i).astype(F32)).astype(F32)
        step_x = tau - pltpu.roll(tau, 1, 0)
        step_y = tau - jnp.where(first, 0.0, pltpu.roll(tau, 1, 1))
        flat_x = jnp.log(1.0 + jnp.exp(-jnp.abs(step_x)))
        flat_y = jnp.log(1.0 + jnp.exp(-jnp.abs(step_y)))
        edge = tau[:, rows - 128 :]
        edge = jnp.maximum(edge, 0.0) + jnp.log(1.0 + jnp.exp(-jnp.abs(edge)))
        west = jnp.maximum(step_x, 0.0) + flat_x
        east = pltpu.roll(jnp.maximum(-step_x, 0.0) + flat_x, count - 1, 0)
        north = jnp.maximum(step_y, 0.0) + flat_y
        south = pltpu.roll(jnp.maximum(-step_y, 0.0) + flat_y, rows - 1, 1)
        edge = jnp.where(last[:, rows - 128 :], edge, south[:, rows - 128 :])
        south = jnp.concatenate([south[:, : rows - 128], edge], axis=1)
        scale = active / (slow + west + east + north + south + window(3, i))
        src_o[i] = scale * window(1, i)
        mid_o[i] = scale * slow
        west_o[i] = scale * west
        east_o[i] = scale * east
        north_o[i] = jnp.where(first, 0.0, scale * north)
        south_o[i] = jnp.where(last, 0.0, scale * south)


def trim(level, cut):
    return level[cut : level.shape[0] - cut] if cut else level


def march(level, coefs, keep):
    src, mid, west, east, north, south = coefs
    count, rows = src.shape[1:]
    halo = (count - COLS) // 2
    for i in range(HALF):
        need = HALF - 1 - i + keep
        cut = max(halo - (need + SIDE - 1) // SIDE * SIDE, 0)
        span = slice(cut, count - cut)
        if level is None:
            level = src[i, span]
        else:
            wide = level.shape[0]
            down, up = pltpu.roll(level, 1, 0), pltpu.roll(level, wide - 1, 0)
            before, after = pltpu.roll(level, 1, 1), pltpu.roll(level, rows - 1, 1)
            lose = (wide - (count - 2 * cut)) // 2
            level, down, up, before, after = (trim(v, lose) for v in (level, down, up, before, after))
            level = (
                src[i, span]
                + mid[i, span] * level
                + west[i, span] * down
                + east[i, span] * up
                + north[i, span] * before
                + south[i, span] * after
            )
        yield level


def sweep_kernel(turn, half, nlevels, *refs):
    count = 12 if half is None else 6
    coefs = refs[:count]
    levels = refs[count : count + nlevels]
    buf_ref, sems = refs[-2:]
    outs = refs[:-2]
    end_ref = None
    if turn is not None:
        end_ref, outs = outs[-1], outs[:-1]
    keep_ref, give_ref = outs[-2:]
    stage, core = place()
    here = 0 if half is not None else (turn if turn is not None else lax.axis_size("sweep") // 2 - 1)

    def send(part, slot, wait):
        @pl.when(core == part)
        def _():
            copy = pltpu.make_async_copy(buf_ref.at[slot], keep_ref, sems.at[slot])
            copy.wait() if wait else copy.start()

        @pl.when(core != part)
        def _():
            copy = pltpu.make_async_copy(buf_ref.at[slot], give_ref, sems.at[slot])
            copy.wait() if wait else copy.start()

    @pl.when(stage == here)
    def _():
        level = None
        if levels:
            low, own, high = (r[...] for r in levels)
            if half is not None:
                low, high = low[SIDE:], high[:SIDE]
            level = jnp.concatenate([low, own, high], axis=0)
        parts = [(half, coefs, 0)] if half is not None else [(0, coefs[:6], HALF), (1, coefs[6:], 0)]
        for slot, (part, own_coefs, keep) in enumerate(parts):
            for i, plane in enumerate(march(level, own_coefs, keep)):
                level = plane
                margin = (level.shape[0] - COLS) // 2
                buf_ref[slot, i] = level[margin : margin + COLS]
            send(part, slot, False)
        if end_ref is not None:
            margin = (level.shape[0] - COLS) // 2
            end_ref[...] = level[margin : margin + COLS]
        for slot, (part, _, _) in enumerate(parts):
            send(part, slot, True)


def finish_kernel(kept_ref, got_ref, slow_ref, adjoint_ref, gradient_ref):
    _, core = place()
    own, got = kept_ref[...], got_ref[...]
    adjoint_ref[core] = own
    adjoint_ref[1 - core] = got
    gradient_ref[...] = slow_ref[...] * (own + got)


def shards(traveltime, residual, slowness, attenuation, topography):
    columns, crosses = topography.shape
    sweeps, lats = lax.axis_size("sweep"), lax.axis_size("lat")
    stages = sweeps // 2
    hbm = pl.BlockSpec(memory_space=pltpu.HBM)
    block = (HALF, columns, crosses)

    def shape(*dims):
        return jax.ShapeDtypeStruct(dims, F32)

    def call(kernel, outs, ins, vmem=4 << 20, in_specs=None, out_specs=None, **kw):
        return pl.pallas_call(
            kernel,
            out_shape=outs,
            in_specs=in_specs or whole(len(ins)),
            out_specs=out_specs or whole(len(outs)),
            compiler_params=pltpu.CompilerParams(vmem_limit_bytes=vmem),
            **kw,
        )(*ins)

    swap = [(i, i ^ 1) for i in range(sweeps)]
    near, away = call(
        split_kernel,
        (shape(4, *block),) * 2,
        (traveltime, residual, slowness, attenuation),
        vmem=60 << 20,
        in_specs=[hbm] * 4,
        scratch_shapes=[pltpu.SemaphoreType.DMA((8,))],
    )
    got = lax.ppermute(away, "sweep", swap)
    (landed,) = call(
        land_kernel,
        (shape(4, *block),),
        (near,),
        in_specs=[hbm],
        scratch_shapes=[pltpu.SemaphoreType.DMA],
        cost_estimate=pl.CostEstimate(flops=0, bytes_accessed=2 << 20, transcendentals=0),
    )
    edges = shape(4 * EDGE + SIDE, crosses)
    mid, *packs = call(pack_kernel, (shape(4, DEEP, columns, crosses),) + (edges,) * 4, (topography, landed, got))
    rightward = [(i, i + 1) for i in range(lats - 1)]
    leftward = [(i + 1, i) for i in range(lats - 1)]
    a_west = lax.ppermute(packs[0], "lat", rightward)
    a_east = lax.ppermute(packs[1], "lat", leftward)
    b_west = lax.ppermute(packs[2], "lat", rightward)
    b_east = lax.ppermute(packs[3], "lat", leftward)

    skirt = shape(4 * SKIRT + SIDE, crosses)
    to_right, to_left = call(skirt_kernel, (skirt,) * 2, (mid, topography))
    upper = [i * lats for i in range(2, sweeps)]
    c_west = lax.ppermute(to_right, AXES, [(i + a, i + b) for i in upper for a, b in rightward])
    c_east = lax.ppermute(to_left, AXES, [(i + a, i + b) for i in upper for a, b in leftward])

    def coef(base, width, ins):
        return call(
            functools.partial(coef_kernel, base),
            (shape(HALF, columns + 2 * width, crosses),) * 6,
            (mid, topography, *ins),
            vmem=8 << 20,
            cost_estimate=pl.CostEstimate(flops=10 << 20, bytes_accessed=3 << 20, transcendentals=0),
        )

    def hop(value, turn, ahead, side):
        pairs = []
        for i in (2 * turn, 2 * turn + 1):
            for k in range(lats):
                if 0 <= k + side < lats:
                    pairs.append((i * lats + k, (i + 2 * ahead) * lats + k + side))
        return lax.ppermute(value, AXES, pairs)

    def sweep(turn, half, coefs, levels, fields):
        ins = (*coefs, *levels, *fields)
        ends = () if turn is None else (shape(columns, crosses),)
        slots = 2 if half is None else 1
        at = len(ins) - 2
        keep, give, *end = call(
            functools.partial(sweep_kernel, turn, half, len(levels)),
            (shape(*block), shape(*block)) + ends,
            ins,
            in_specs=whole(len(coefs) + len(levels)) + [hbm] * len(fields),
            out_specs=[hbm, hbm] + whole(len(ends)),
            input_output_aliases={at: 0, at + 1: 1} if fields else {},
            scratch_shapes=[VM((slots, *block), F32), pltpu.SemaphoreType.DMA((2,))],
        )
        return (keep, give), end

    coef_a = coef(0, SIDE, (a_west, a_east))
    fields, (end,) = sweep(0, 0, coef_a, (), ())
    low, high = hop(end, 0, 0, 1), hop(end, 0, 0, -1)
    coef_b = coef(HALF, SIDE, (b_west, b_east))
    fields, (end,) = sweep(0, 1, coef_b, (low, end, high), fields)

    def forward(end, turn):
        low = hop(end, turn, 1, 1)
        high = hop(end, turn, 1, -1)
        own = hop(end, turn, 1, 0)
        return low, own, high

    levels = forward(end, 0)
    coef_c = coef(0, COLS, (a_west, a_east, c_west, c_east))
    for turn in range(1, stages):
        more = turn < stages - 1
        fields, end = sweep(turn if more else None, None, (*coef_c, *coef_b), levels, fields)
        if more:
            levels = forward(end[0], turn)
    keep, give = fields
    given = lax.ppermute(give, "sweep", swap)
    return call(finish_kernel, (shape(2, *block), shape(*block)), (keep, given, slowness))


def solution(mesh):
    in_specs = (
        P(None, "sweep", "lat", None),
        P(None, "sweep", "lat", None),
        P("sweep", "lat", None),
        P("sweep", "lat", None),
        P("lat", None),
    )
    out_specs = (P(None, "sweep", "lat", None), P("sweep", "lat", None))
    return jax.shard_map(shards, mesh=mesh, in_specs=in_specs, out_specs=out_specs, check_vma=False)
```

time: 110 us -> 112 us (1.018)
  starting transfers between devices: 36.8 us -> 52.2 us
  waiting for transfers between devices: 62.1 us -> 48.1 us
    ppermute x2 -> x6, starting transfers between devices: 8.6 us -> 22.5 us  [the longest x1 5.48 us: shards(): lax.ppermute(to_left, AXES, [(i + a, i + b) for i in upper for a, b in le...]
    ppermute x2 -> x6, waiting for transfers between devices: 17.8 us -> 5.84 us  [the longest x1 3.32 us: shards(): b_east = lax.ppermute(packs[3], 'lat', leftward)]
    ppermute x21 -> x23, starting transfers between devices: 15.8 us -> 17.1 us  [hop(): return lax.ppermute(value, AXES, pairs)]
    ppermute x1, waiting for transfers between devices: 2.1 us -> 0.89 us  [shards(): got = lax.ppermute(away, 'sweep', swap)]
    ppermute x21 -> x23, waiting for transfers between devices: 41.1 us -> 40.3 us  [hop(): return lax.ppermute(value, AXES, pairs)]
    pallas_call x12 -> x17, Pallas kernels: 8.6 us -> 8.89 us  [call(): pl.pallas_call(kernel, out_shape=outs, in_specs=in_specs or whole(len(ins...]
  transfers between devices with their start and end apart: 25 -> 31, of which waited for: 7 -> 7; matrix products, arithmetic and copies ran while one was open for 0% -> 0% of each run, Pallas kernels for 0% -> 3%
where the time goes in v2:
time: 112 us
  starting transfers between devices  52.2 us (47%)
  waiting for transfers between devices  48.1 us (43%)
  Pallas kernels  8.89 us (8%)
  between operations  1.21 us (1%)
  local copies, waits for them, and re-layouts  1.13 us (1%)
    ppermute x23, waiting for transfers between devices, hop(): return lax.ppermute(value, AXES, pairs)  40.3 us
    ppermute x23, starting transfers between devices, hop(): return lax.ppermute(value, AXES, pairs)  17.1 us
    ppermute x1, starting transfers between devices, shards(): given = lax.ppermute(give, 'sweep', swap)  10 us
    pallas_call x17, Pallas kernels, call(): pl.pallas_call(kernel, out_shape=outs, in_specs=in_specs or whole(len(ins...  8.89 us
    ppermute x1, starting transfers between devices, shards(): lax.ppermute(to_left, AXES, [(i + a, i + b) for i in upper for a, b in le...  5.48 us
    ppermute x1, starting transfers between devices, shards(): b_east = lax.ppermute(packs[3], 'lat', leftward)  5.48 us
    ppermute x1, waiting for transfers between devices, shards(): b_east = lax.ppermute(packs[3], 'lat', leftward)  3.32 us
    ppermute x1, starting transfers between devices, shards(): a_west = lax.ppermute(packs[0], 'lat', rightward)  3.12 us
  transfers between devices with their start and end apart: 31, of which 7 were waited for; matrix products, arithmetic and copies ran while one was open for 0% of the time, Pallas kernels for 3%

profile of v2, /device:TPU:481, one launch (start us, length us, event | category | flops | bytes accessed | tf_op | source)
XLA Modules:
  0.0 111.6 jit_solution(24802033840425182)
XLA Ops:
  0.6 2.7 %shard_map.68 = (f32[4,8,16,384]{3,2,1,0:T(8,128)}, f32[4,8,16,384]{3,2,1,0:T(8,128)}) custom-call(f32[2,8,16,384]{3,2,1,0:T(8,128)} %tau.1, f32[2,8,16,384]{3,2,1,0:T(8,128)} %res.1, f32[8,16,384]{2,1,0:T(8,128)} %slow_ref.1, f32[8,16,384]{2,1,0:T(8,128)} %att.1), custom_call_target="tpu_custom_call" | custom-call | tf_op jit(solution)/shard_map/pallas_call | solution.py:245
  3.4 2.6 %collective-permute-start = (f32[4,8,16,384]{3,2,1,0:T(8,128)}, f32[4,8,16,384]{3,2,1,0:T(8,128)S(1)}, u32[]{:S(2)}, u32[]{:S(2)}) collective-permute-start(f32[4,8,16,384]{3,2,1,0:T(8,128)} %get-tuple-element.56), channel_id=1, source_target_pairs={{0,32},{32,0},{64,96},{96,64},{128,160},{160,128},{192,224},{224,1... | collective-permute-start | bytes 2359304 | tf_op jit(solution)/shard_map/ppermute | solution.py:263
  6.0 1.1 %copy-done = f32[4,8,16,384]{3,2,1,0:T(8,128)S(1)} copy-done((f32[4,8,16,384]{3,2,1,0:T(8,128)S(1)}, f32[4,8,16,384]{3,2,1,0:T(8,128)}, u32[]{:S(2)}) %copy-start) | copy-done | bytes 786456
  7.2 0.9 collective-permute-done.got_ref
  8.3 3.1 %collective-permute-start.1 = (f32[168,384]{1,0:T(8,128)S(1)}, f32[168,384]{1,0:T(8,128)S(1)}, u32[]{:S(2)}, u32[]{:S(2)}) collective-permute-start(f32[168,384]{1,0:T(8,128)S(1)} %get-tuple-element.58), channel_id=1, source_target_pairs={{0,1},{1,2},{2,3},{3,4},{4,5},{5,6},{6,7},{7,8},{8,9},{9,10},{10,1... | collective-permute-start | bytes 774152 | tf_op jit(solution)/shard_map/ppermute | solution.py:276
  11.5 3.1 %collective-permute-start.3 = (f32[264,384]{1,0:T(8,128)S(1)}, f32[264,384]{1,0:T(8,128)S(1)}, u32[]{:S(2)}, u32[]{:S(2)}) collective-permute-start(f32[264,384]{1,0:T(8,128)S(1)} %get-tuple-element.60), channel_id=1, source_target_pairs={{64,65},{65,66},{66,67},{67,68},{68,69},{69,70},{70,71},{71,72},{7... | collective-permute-start | bytes 1216520 | tf_op jit(solution)/shard_map/ppermute | solution.py:284
  14.6 5.5 %collective-permute-start.4 = (f32[264,384]{1,0:T(8,128)S(1)}, f32[264,384]{1,0:T(8,128)S(1)}, u32[]{:S(2)}, u32[]{:S(2)}) collective-permute-start(f32[264,384]{1,0:T(8,128)S(1)} %get-tuple-element.61), channel_id=1, source_target_pairs={{65,64},{66,65},{67,66},{68,67},{69,68},{70,69},{71,70},{72,71},{7... | collective-permute-start | bytes 1216520 | tf_op jit(solution)/shard_map/ppermute | solution.py:285
  20.1 2.2 %collective-permute-start.2 = (f32[168,384]{1,0:T(8,128)S(1)}, f32[168,384]{1,0:T(8,128)S(1)}, u32[]{:S(2)}, u32[]{:S(2)}) collective-permute-start(f32[168,384]{1,0:T(8,128)S(1)} %get-tuple-element.59), channel_id=1, source_target_pairs={{1,0},{2,1},{3,2},{4,3},{5,4},{6,5},{7,6},{8,7},{9,8},{10,9},{11,1... | collective-permute-start | bytes 774152 | tf_op jit(solution)/shard_map/ppermute | solution.py:277
  22.3 3.1 %collective-permute-start.5 = (f32[168,384]{1,0:T(8,128)S(1)}, f32[168,384]{1,0:T(8,128)S(1)}, u32[]{:S(2)}, u32[]{:S(2)}) collective-permute-start(f32[168,384]{1,0:T(8,128)S(1)} %get-tuple-element.68), channel_id=1, source_target_pairs={{0,1},{1,2},{2,3},{3,4},{4,5},{5,6},{6,7},{7,8},{8,9},{9,10},{10,1... | collective-permute-start | bytes 774152 | tf_op jit(solution)/shard_map/ppermute | solution.py:278
  25.4 5.5 %collective-permute-start.6 = (f32[168,384]{1,0:T(8,128)S(1)}, f32[168,384]{1,0:T(8,128)S(1)}, u32[]{:S(2)}, u32[]{:S(2)}) collective-permute-start(f32[168,384]{1,0:T(8,128)S(1)} %get-tuple-element.69), channel_id=1, source_target_pairs={{1,0},{2,1},{3,2},{4,3},{5,4},{6,5},{7,6},{8,7},{9,8},{10,9},{11,1... | collective-permute-start | bytes 774152 | tf_op jit(solution)/shard_map/ppermute | solution.py:279
  30.9 2.5 %collective-permute-done.2.east_ref = f32[168,384]{1,0:T(8,128)S(1)} collective-permute-done((f32[168,384]{1,0:T(8,128)S(1)}, f32[168,384]{1,0:T(8,128)S(1)}, u32[]{:S(2)}, u32[]{:S(2)}) %collective-permute-start.2) | collective-permute-done | bytes 258080 | tf_op jit(solution)/shard_map/ppermute | solution.py:277
  33.4 0.8 shard_map.74
  35.6 3.3 %collective-permute-done.6.east_ref = f32[168,384]{1,0:T(8,128)S(1)} collective-permute-done((f32[168,384]{1,0:T(8,128)S(1)}, f32[168,384]{1,0:T(8,128)S(1)}, u32[]{:S(2)}, u32[]{:S(2)}) %collective-permute-start.6) | collective-permute-done | bytes 258080 | tf_op jit(solution)/shard_map/ppermute | solution.py:279
  41.8 1.2 %shard_map.72 = (f32[8,48,384]{2,1,0:T(8,128)S(1)}, f32[8,48,384]{2,1,0:T(8,128)S(1)}, f32[8,48,384]{2,1,0:T(8,128)S(1)}, f32[8,48,384]{2,1,0:T(8,128)S(1)}, f32...) custom-call(f32[4,16,16,384]{3,2,1,0:T(8,128)S(1)} %get-tuple-element.57.mid_ref, s32[16,384]{1,0:T(8,128)S(1)} %copy-done.2, ...), custom_call_target="tpu_custom_call" | custom-call | flops 10485760 | bytes 3145728 | tf_op jit(solution)/shard_map/pallas_call | solution.py:245
  53.6 1.3 %collective-permute-start.29 = (f32[16,384]{1,0:T(8,128)S(1)}, f32[16,384]{1,0:T(8,128)S(1)}, u32[]{:S(2)}, u32[]{:S(2)}) collective-permute-start(f32[16,384]{1,0:T(8,128)S(1)} %get-tuple-element.103), channel_id=1, source_target_pairs={{385,448},{386,449},{387,450},{388,451},{389,452},{390,453},{391,4... | collective-permute-start | bytes 73736 | tf_op jit(solution)/shard_map/ppermute | solution.py:302
  54.9 1.3 %collective-permute-start.28 = (f32[16,384]{1,0:T(8,128)S(1)}, f32[16,384]{1,0:T(8,128)S(1)}, u32[]{:S(2)}, u32[]{:S(2)}) collective-permute-start(f32[16,384]{1,0:T(8,128)S(1)} %get-tuple-element.103), channel_id=1, source_target_pairs={{384,448},{385,449},{386,450},{387,451},{388,452},{389,453},{390,4... | collective-permute-start | bytes 73736 | tf_op jit(solution)/shard_map/ppermute | solution.py:302
  56.2 1.3 %collective-permute-start.27 = (f32[16,384]{1,0:T(8,128)S(1)}, f32[16,384]{1,0:T(8,128)S(1)}, u32[]{:S(2)}, u32[]{:S(2)}) collective-permute-start(f32[16,384]{1,0:T(8,128)S(1)} %get-tuple-element.103), channel_id=1, source_target_pairs={{384,449},{385,450},{386,451},{387,452},{388,453},{389,454},{390,4... | collective-permute-start | bytes 73736 | tf_op jit(solution)/shard_map/ppermute | solution.py:302
  57.5 36.9 %collective-permute-done.29.refs_14_ = f32[16,384]{1,0:T(8,128)S(1)} collective-permute-done((f32[16,384]{1,0:T(8,128)S(1)}, f32[16,384]{1,0:T(8,128)S(1)}, u32[]{:S(2)}, u32[]{:S(2)}) %collective-permute-start.29) | collective-permute-done | bytes 24608 | tf_op jit(solution)/shard_map/ppermute | solution.py:302
  94.4 2.1 %collective-permute-done.28.refs_13_ = f32[16,384]{1,0:T(8,128)S(1)} collective-permute-done((f32[16,384]{1,0:T(8,128)S(1)}, f32[16,384]{1,0:T(8,128)S(1)}, u32[]{:S(2)}, u32[]{:S(2)}) %collective-permute-start.28) | collective-permute-done | bytes 24608 | tf_op jit(solution)/shard_map/ppermute | solution.py:302
  96.5 1.2 %collective-permute-done.27.refs_12_ = f32[16,384]{1,0:T(8,128)S(1)} collective-permute-done((f32[16,384]{1,0:T(8,128)S(1)}, f32[16,384]{1,0:T(8,128)S(1)}, u32[]{:S(2)}, u32[]{:S(2)}) %collective-permute-start.27) | collective-permute-done | bytes 24608 | tf_op jit(solution)/shard_map/ppermute | solution.py:302
  97.8 1.8 %shard_map.83 = (f32[8,16,384]{2,1,0:T(8,128)S(1)}, f32[8,16,384]{2,1,0:T(8,128)S(1)}) custom-call(f32[8,48,384]{2,1,0:T(8,128)S(1)} %get-tuple-element.62.refs_0_, f32[8,48,384]{2,1,0:T(8,128)S(1)} %get-tuple-element.63.refs_1_, f32[8,48,384]{2,1,0:T(8,128)S(1)} %get-tuple-element.64.refs_2_, ...), custom_call_target="tpu_custom_call", output_to_operand_aliasing={{0}: (15, {}), {1}: (16, {})} | custom-call | tf_op jit(solution)/shard_map/pallas_call | solution.py:245
  99.6 10.0 %collective-permute-start.30 = (f32[8,16,384]{2,1,0:T(8,128)S(1)}, f32[8,16,384]{2,1,0:T(8,128)S(1)}, u32[]{:S(2)}, u32[]{:S(2)}) collective-permute-start(f32[8,16,384]{2,1,0:T(8,128)S(1)} %get-tuple-element.107), channel_id=1, source_target_pairs={{0,32},{32,0},{64,96},{96,64},{128,160},{160,128},{192,224},{224,1... | collective-permute-start | bytes 589832 | tf_op jit(solution)/shard_map/ppermute | solution.py:340
  109.6 1.0 collective-permute-done.30.got_ref
  110.7 0.9 shard_map.84
  (61 shorter events, 14.8 us)
Async XLA Ops:
  3.4 4.7 %collective-permute-start = (f32[4,8,16,384]{3,2,1,0:T(8,128)}, f32[4,8,16,384]{3,2,1,0:T(8,128)S(1)}, u32[]{:S(2)}, u32[]{:S(2)}) collective-permute-start(f32[4,8,16,384]{3,2,1,0:T(8,128)} %get-tuple-element.56), channel_id=1, source_target_pairs={{0,32},{32,0},{64,96},{96,64},{128,160},{160,128},{192,224},{224,1... | collective-permute-start | bytes 2359304 | tf_op jit(solution)/shard_map/ppermute | solution.py:263
  8.3 17.1 %collective-permute-start.1 = (f32[168,384]{1,0:T(8,128)S(1)}, f32[168,384]{1,0:T(8,128)S(1)}, u32[]{:S(2)}, u32[]{:S(2)}) collective-permute-start(f32[168,384]{1,0:T(8,128)S(1)} %get-tuple-element.58), channel_id=1, source_target_pairs={{0,1},{1,2},{2,3},{3,4},{4,5},{5,6},{6,7},{7,8},{8,9},{9,10},{10,1... | collective-permute-start | bytes 774152 | tf_op jit(solution)/shard_map/ppermute | solution.py:276
  11.5 30.3 %collective-permute-start.3 = (f32[264,384]{1,0:T(8,128)S(1)}, f32[264,384]{1,0:T(8,128)S(1)}, u32[]{:S(2)}, u32[]{:S(2)}) collective-permute-start(f32[264,384]{1,0:T(8,128)S(1)} %get-tuple-element.60), channel_id=1, source_target_pairs={{64,65},{65,66},{66,67},{67,68},{68,69},{69,70},{70,71},{71,72},{7... | collective-permute-start | bytes 1216520 | tf_op jit(solution)/shard_map/ppermute | solution.py:284
  14.6 27.2 %collective-permute-start.4 = (f32[264,384]{1,0:T(8,128)S(1)}, f32[264,384]{1,0:T(8,128)S(1)}, u32[]{:S(2)}, u32[]{:S(2)}) collective-permute-start(f32[264,384]{1,0:T(8,128)S(1)} %get-tuple-element.61), channel_id=1, source_target_pairs={{65,64},{66,65},{67,66},{68,67},{69,68},{70,69},{71,70},{72,71},{7... | collective-permute-start | bytes 1216520 | tf_op jit(solution)/shard_map/ppermute | solution.py:285
  20.1 13.3 %collective-permute-start.2 = (f32[168,384]{1,0:T(8,128)S(1)}, f32[168,384]{1,0:T(8,128)S(1)}, u32[]{:S(2)}, u32[]{:S(2)}) collective-permute-start(f32[168,384]{1,0:T(8,128)S(1)} %get-tuple-element.59), channel_id=1, source_target_pairs={{1,0},{2,1},{3,2},{4,3},{5,4},{6,5},{7,6},{8,7},{9,8},{10,9},{11,1... | collective-permute-start | bytes 774152 | tf_op jit(solution)/shard_map/ppermute | solution.py:277
  22.3 12.7 %collective-permute-start.5 = (f32[168,384]{1,0:T(8,128)S(1)}, f32[168,384]{1,0:T(8,128)S(1)}, u32[]{:S(2)}, u32[]{:S(2)}) collective-permute-start(f32[168,384]{1,0:T(8,128)S(1)} %get-tuple-element.68), channel_id=1, source_target_pairs={{0,1},{1,2},{2,3},{3,4},{4,5},{5,6},{6,7},{7,8},{8,9},{9,10},{10,1... | collective-permute-start | bytes 774152 | tf_op jit(solution)/shard_map/ppermute | solution.py:278
  25.4 13.5 %collective-permute-start.6 = (f32[168,384]{1,0:T(8,128)S(1)}, f32[168,384]{1,0:T(8,128)S(1)}, u32[]{:S(2)}, u32[]{:S(2)}) collective-permute-start(f32[168,384]{1,0:T(8,128)S(1)} %get-tuple-element.69), channel_id=1, source_target_pairs={{1,0},{2,1},{3,2},{4,3},{5,4},{6,5},{7,6},{8,7},{9,8},{10,9},{11,1... | collective-permute-start | bytes 774152 | tf_op jit(solution)/shard_map/ppermute | solution.py:279
  34.2 5.5 %collective-permute-start.8 = (f32[16,384]{1,0:T(8,128)S(1)}, f32[16,384]{1,0:T(8,128)S(1)}, u32[]{:S(2)}, u32[]{:S(2)}) collective-permute-start(f32[16,384]{1,0:T(8,128)S(1)} %get-tuple-element.82.refs_7_), channel_id=1, source_target_pairs={{1,0},{2,1},{3,2},{4,3},{5,4},{6,5},{7,6},{8,7},{9,8},{10,9},{11,1... | collective-permute-start | bytes 73736 | tf_op jit(solution)/shard_map/ppermute | solution.py:302
  34.9 4.8 %collective-permute-start.7 = (f32[16,384]{1,0:T(8,128)S(1)}, f32[16,384]{1,0:T(8,128)S(1)}, u32[]{:S(2)}, u32[]{:S(2)}) collective-permute-start(f32[16,384]{1,0:T(8,128)S(1)} %get-tuple-element.82.refs_7_), channel_id=1, source_target_pairs={{0,1},{1,2},{2,3},{3,4},{4,5},{5,6},{6,7},{7,8},{8,9},{9,10},{10,1... | collective-permute-start | bytes 73736 | tf_op jit(solution)/shard_map/ppermute | solution.py:302
  39.8 3.2 %collective-permute-start.11 = (f32[16,384]{1,0:T(8,128)S(1)}, f32[16,384]{1,0:T(8,128)S(1)}, u32[]{:S(2)}, u32[]{:S(2)}) collective-permute-start(f32[16,384]{1,0:T(8,128)S(1)} %get-tuple-element.85), channel_id=1, source_target_pairs={{1,64},{2,65},{3,66},{4,67},{5,68},{6,69},{7,70},{8,71},{9,72},{10... | collective-permute-start | bytes 73736 | tf_op jit(solution)/shard_map/ppermute | solution.py:302
  40.5 2.6 %collective-permute-start.10 = (f32[16,384]{1,0:T(8,128)S(1)}, f32[16,384]{1,0:T(8,128)S(1)}, u32[]{:S(2)}, u32[]{:S(2)}) collective-permute-start(f32[16,384]{1,0:T(8,128)S(1)} %get-tuple-element.85), channel_id=1, source_target_pairs={{0,64},{1,65},{2,66},{3,67},{4,68},{5,69},{6,70},{7,71},{8,72},{9,... | collective-permute-start | bytes 73736 | tf_op jit(solution)/shard_map/ppermute | solution.py:302
  41.1 1.9 %collective-permute-start.9 = (f32[16,384]{1,0:T(8,128)S(1)}, f32[16,384]{1,0:T(8,128)S(1)}, u32[]{:S(2)}, u32[]{:S(2)}) collective-permute-start(f32[16,384]{1,0:T(8,128)S(1)} %get-tuple-element.85), channel_id=1, source_target_pairs={{0,65},{1,66},{2,67},{3,68},{4,69},{5,70},{6,71},{7,72},{8,73},{9,... | collective-permute-start | bytes 73736 | tf_op jit(solution)/shard_map/ppermute | solution.py:302
  43.1 2.0 %collective-permute-start.14 = (f32[16,384]{1,0:T(8,128)S(1)}, f32[16,384]{1,0:T(8,128)S(1)}, u32[]{:S(2)}, u32[]{:S(2)}) collective-permute-start(f32[16,384]{1,0:T(8,128)S(1)} %get-tuple-element.88), channel_id=1, source_target_pairs={{65,128},{66,129},{67,130},{68,131},{69,132},{70,133},{71,134},{72... | collective-permute-start | bytes 73736 | tf_op jit(solution)/shard_map/ppermute | solution.py:302
  43.8 1.4 %collective-permute-start.13 = (f32[16,384]{1,0:T(8,128)S(1)}, f32[16,384]{1,0:T(8,128)S(1)}, u32[]{:S(2)}, u32[]{:S(2)}) collective-permute-start(f32[16,384]{1,0:T(8,128)S(1)} %get-tuple-element.88), channel_id=1, source_target_pairs={{64,128},{65,129},{66,130},{67,131},{68,132},{69,133},{70,134},{71... | collective-permute-start | bytes 73736 | tf_op jit(solution)/shard_map/ppermute | solution.py:302
  45.2 2.0 %collective-permute-start.17 = (f32[16,384]{1,0:T(8,128)S(1)}, f32[16,384]{1,0:T(8,128)S(1)}, u32[]{:S(2)}, u32[]{:S(2)}) collective-permute-start(f32[16,384]{1,0:T(8,128)S(1)} %get-tuple-element.91), channel_id=1, source_target_pairs={{129,192},{130,193},{131,194},{132,195},{133,196},{134,197},{135,1... | collective-permute-start | bytes 73736 | tf_op jit(solution)/shard_map/ppermute | solution.py:302
  47.3 2.0 %collective-permute-start.20 = (f32[16,384]{1,0:T(8,128)S(1)}, f32[16,384]{1,0:T(8,128)S(1)}, u32[]{:S(2)}, u32[]{:S(2)}) collective-permute-start(f32[16,384]{1,0:T(8,128)S(1)} %get-tuple-element.94), channel_id=1, source_target_pairs={{193,256},{194,257},{195,258},{196,259},{197,260},{198,261},{199,2... | collective-permute-start | bytes 73736 | tf_op jit(solution)/shard_map/ppermute | solution.py:302
  48.0 1.4 %collective-permute-start.19 = (f32[16,384]{1,0:T(8,128)S(1)}, f32[16,384]{1,0:T(8,128)S(1)}, u32[]{:S(2)}, u32[]{:S(2)}) collective-permute-start(f32[16,384]{1,0:T(8,128)S(1)} %get-tuple-element.94), channel_id=1, source_target_pairs={{192,256},{193,257},{194,258},{195,259},{196,260},{197,261},{198,2... | collective-permute-start | bytes 73736 | tf_op jit(solution)/shard_map/ppermute | solution.py:302
  49.4 2.0 %collective-permute-start.23 = (f32[16,384]{1,0:T(8,128)S(1)}, f32[16,384]{1,0:T(8,128)S(1)}, u32[]{:S(2)}, u32[]{:S(2)}) collective-permute-start(f32[16,384]{1,0:T(8,128)S(1)} %get-tuple-element.97), channel_id=1, source_target_pairs={{257,320},{258,321},{259,322},{260,323},{261,324},{262,325},{263,3... | collective-permute-start | bytes 73736 | tf_op jit(solution)/shard_map/ppermute | solution.py:302
  51.5 2.0 %collective-permute-start.26 = (f32[16,384]{1,0:T(8,128)S(1)}, f32[16,384]{1,0:T(8,128)S(1)}, u32[]{:S(2)}, u32[]{:S(2)}) collective-permute-start(f32[16,384]{1,0:T(8,128)S(1)} %get-tuple-element.100), channel_id=1, source_target_pairs={{321,384},{322,385},{323,386},{324,387},{325,388},{326,389},{327,3... | collective-permute-start | bytes 73736 | tf_op jit(solution)/shard_map/ppermute | solution.py:302
  52.2 1.4 %collective-permute-start.25 = (f32[16,384]{1,0:T(8,128)S(1)}, f32[16,384]{1,0:T(8,128)S(1)}, u32[]{:S(2)}, u32[]{:S(2)}) collective-permute-start(f32[16,384]{1,0:T(8,128)S(1)} %get-tuple-element.100), channel_id=1, source_target_pairs={{320,384},{321,385},{322,386},{323,387},{324,388},{325,389},{326,3... | collective-permute-start | bytes 73736 | tf_op jit(solution)/shard_map/ppermute | solution.py:302
  53.6 40.8 %collective-permute-start.29 = (f32[16,384]{1,0:T(8,128)S(1)}, f32[16,384]{1,0:T(8,128)S(1)}, u32[]{:S(2)}, u32[]{:S(2)}) collective-permute-start(f32[16,384]{1,0:T(8,128)S(1)} %get-tuple-element.103), channel_id=1, source_target_pairs={{385,448},{386,449},{387,450},{388,451},{389,452},{390,453},{391,4... | collective-permute-start | bytes 73736 | tf_op jit(solution)/shard_map/ppermute | solution.py:302
  54.9 41.6 %collective-permute-start.28 = (f32[16,384]{1,0:T(8,128)S(1)}, f32[16,384]{1,0:T(8,128)S(1)}, u32[]{:S(2)}, u32[]{:S(2)}) collective-permute-start(f32[16,384]{1,0:T(8,128)S(1)} %get-tuple-element.103), channel_id=1, source_target_pairs={{384,448},{385,449},{386,450},{387,451},{388,452},{389,453},{390,4... | collective-permute-start | bytes 73736 | tf_op jit(solution)/shard_map/ppermute | solution.py:302
  56.2 41.6 %collective-permute-start.27 = (f32[16,384]{1,0:T(8,128)S(1)}, f32[16,384]{1,0:T(8,128)S(1)}, u32[]{:S(2)}, u32[]{:S(2)}) collective-permute-start(f32[16,384]{1,0:T(8,128)S(1)} %get-tuple-element.103), channel_id=1, source_target_pairs={{384,449},{385,450},{386,451},{387,452},{388,453},{389,454},{390,4... | collective-permute-start | bytes 73736 | tf_op jit(solution)/shard_map/ppermute | solution.py:302
  99.6 11.1 %collective-permute-start.30 = (f32[8,16,384]{2,1,0:T(8,128)S(1)}, f32[8,16,384]{2,1,0:T(8,128)S(1)}, u32[]{:S(2)}, u32[]{:S(2)}) collective-permute-start(f32[8,16,384]{2,1,0:T(8,128)S(1)} %get-tuple-element.107), channel_id=1, source_target_pairs={{0,32},{32,0},{64,96},{96,64},{128,160},{160,128},{192,224},{224,1... | collective-permute-start | bytes 589832 | tf_op jit(solution)/shard_map/ppermute | solution.py:340
  (10 other events, 27.7 us)
